TPU v7x, 32 devices: a whole 2x2x4 slice. The times are simulated.
32 devices in a mesh: aa: 4 (over z), ba: 8 (over y, x, core).
Axes of the slice: x: 2, y: 2, z: 4, core: 2. Of those that a mesh axis runs over, the one named last changes fastest.
Arguments:
- atom_cond: float32 [12288, 128], P(('aa', 'ba')), may hold values from -6 to 6
- noisy_pos: float32 [3, 12288], P(None, ('aa', 'ba')), may hold values from -8 to 8
- noise_level: float32 [1], replicated, may hold values from 0.1 to 4
- atom_token: int32 [12288], P(('aa', 'ba')), may hold values from -1 to 1023, as said below
- token_cond: float32 [1024, 768], P('aa'), may hold values from -6 to 6
- pair: bfloat16 [1024, 1024, 128], P('aa', 'ba'), may hold values from -64 to 64
- pair_bias_weight: bfloat16 [16, 128], replicated, may hold values from -0.375 to 0.375
- gains: float32 [3, 768], replicated, may hold values from 0.25 to 1.75
- w_pos: float32 [3, 128], replicated, may hold values from -3.5 to 3.5
- w_atom_token: bfloat16 [128, 768], replicated, may hold values from -0.5 to 0.5
- w_query_gate: bfloat16 [768, 1536], replicated, may hold values from -0.21875 to 0.21875
- w_key_value: bfloat16 [768, 1536], replicated, may hold values from -0.21875 to 0.21875
- w_attn_out: bfloat16 [768, 768], replicated, may hold values from -0.21875 to 0.21875
- w_up: bfloat16 [768, 3072], replicated, may hold values from -0.21875 to 0.21875
- w_down: bfloat16 [1536, 768], replicated, may hold values from -0.15625 to 0.15625
- w_token_atom: bfloat16 [768, 128], replicated, may hold values from -0.21875 to 0.21875
- w_pos_out: bfloat16 [3, 128], replicated, may hold values from -0.5 to 0.5
Outputs:
- denoised: float32 [3, 12288], P(None, ('aa', 'ba'))
- token_out: float32 [1024, 768], P('aa')
Inputs may be any that keep to these rules, and one draw needn't show every extreme that they name: `atom_token`: atom slots come in 4 groups of 3072 consecutive slots; group r holds only atoms of tokens r * 256 to (r + 1) * 256 - 1, in nondecreasing token order, live slots first and -1 after them. Every token has 1 to 12 atoms, and some token of every group has exactly 12.
All inputs are finite; a program needn't handle non-finite values.
Results may differ from a plain program's by a relative error of at most 0.01.
Values may be sent and summed in bfloat16 or wider, within the bound.
A program may use at most 128 MiB of HBM per device.

v0:
```python
import functools

import jax
import jax.numpy as jnp
from jax import lax
from jax.experimental import pallas as pl
from jax.experimental.pallas import tpu as pltpu
from jax.sharding import PartitionSpec as P

D = 768
HEADS = 16
MESH = pl.DeviceIdType.MESH


def exchange(arrays, axis, n, scatter, collective_id):
    count = len(arrays)

    def kernel(*refs):
        ins, outs = refs[:count], refs[count : 2 * count]
        local_sem, send_sem, recv_sem = refs[2 * count :]
        me = lax.axis_index(axis)
        barrier = pltpu.get_barrier_semaphore()
        for k in range(1, n):
            pl.semaphore_signal(
                barrier, inc=1, device_id={axis: lax.rem(me + k, n)}, device_id_type=MESH
            )
        own = []
        for a in range(count):
            src = ins[a].at[me] if scatter else ins[a]
            own.append(pltpu.make_async_copy(src, outs[a].at[me], local_sem.at[a]))
            own[-1].start()
        pl.semaphore_wait(barrier, n - 1)
        copies = []
        for k in range(1, n):
            peer = lax.rem(me + k, n)
            for a in range(count):
                copy = pltpu.make_async_remote_copy(
                    src_ref=ins[a].at[peer] if scatter else ins[a],
                    dst_ref=outs[a].at[me],
                    send_sem=send_sem.at[a, k - 1],
                    recv_sem=recv_sem.at[a, k - 1],
                    device_id={axis: peer},
                    device_id_type=MESH,
                )
                copy.start()
                copies.append(copy)
        for copy in own + copies:
            copy.wait()

    shapes = [x.shape if scatter else (n, *x.shape) for x in arrays]
    return pl.pallas_call(
        kernel,
        out_shape=[jax.ShapeDtypeStruct(s, x.dtype) for s, x in zip(shapes, arrays)],
        in_specs=[pl.BlockSpec(memory_space=pl.ANY)] * count,
        out_specs=[pl.BlockSpec(memory_space=pl.ANY)] * count,
        scratch_shapes=[
            pltpu.SemaphoreType.DMA((count,)),
            pltpu.SemaphoreType.DMA((count, n - 1)),
            pltpu.SemaphoreType.DMA((count, n - 1)),
        ],
        compiler_params=pltpu.CompilerParams(collective_id=collective_id, has_side_effects=True),
    )(*arrays)


def spread(rows, n, per_row, offset_of, collective_id):
    def kernel(in_ref, out_ref, local_sem, send_sem, recv_sem):
        me = lax.axis_index("aa")
        owner = lax.axis_index("ba") * offset_of // per_row
        barrier = pltpu.get_barrier_semaphore()
        for k in range(1, n):
            pl.semaphore_signal(
                barrier, inc=1, device_id={"aa": lax.rem(me + k, n)}, device_id_type=MESH
            )
        pl.semaphore_wait(barrier, n - 1)

        def copy_to(k):
            return pltpu.make_async_remote_copy(
                src_ref=in_ref,
                dst_ref=out_ref,
                send_sem=send_sem.at[k - 1],
                recv_sem=recv_sem,
                device_id={"aa": lax.rem(me + k, n)},
                device_id_type=MESH,
            )

        @pl.when(me == owner)
        def _():
            for k in range(1, n):
                copy_to(k).start()
            own = pltpu.make_async_copy(in_ref, out_ref, local_sem)
            own.start()
            own.wait()
            for k in range(1, n):
                copy_to(k).wait_send()

        @pl.when(me != owner)
        def _():
            copy_to(1).wait_recv()

    return pl.pallas_call(
        kernel,
        out_shape=jax.ShapeDtypeStruct(rows.shape, rows.dtype),
        in_specs=[pl.BlockSpec(memory_space=pl.ANY)],
        out_specs=pl.BlockSpec(memory_space=pl.ANY),
        scratch_shapes=[
            pltpu.SemaphoreType.DMA,
            pltpu.SemaphoreType.DMA((n - 1,)),
            pltpu.SemaphoreType.DMA,
        ],
        compiler_params=pltpu.CompilerParams(collective_id=collective_id, has_side_effects=True),
    )(rows)


def layer_norm(values, gain_row):
    mean_value = jnp.mean(values, axis=-1, keepdims=True)
    centered = values - mean_value
    variance = jnp.mean(centered * centered, axis=-1, keepdims=True)
    return centered * lax.rsqrt(variance + 1e-05) * gain_row


def token_sums(local_ids, rounded_state, w_atom_token, tok_rows):
    selector = (jnp.arange(tok_rows, dtype=jnp.int32)[:, None] == local_ids[None, :]).astype(
        jnp.bfloat16
    )
    hidden_atom = jax.nn.relu(
        jnp.dot(rounded_state, w_atom_token, preferred_element_type=jnp.float32)
    ).astype(jnp.bfloat16)
    sums = lax.dot_general(
        selector, hidden_atom, (((1,), (0,)), ((), ())), preferred_element_type=jnp.float32
    )
    return (sums, jnp.sum(selector.astype(jnp.float32), axis=1))


def project_start(tokens_start, gains, w_query_gate):
    normed = layer_norm(tokens_start, gains[0]).astype(jnp.bfloat16)
    query_gate = jnp.dot(normed, w_query_gate, preferred_element_type=jnp.float32)
    width = query_gate.shape[1] // 2
    query_rows = query_gate[:, :width].astype(jnp.bfloat16)
    gate_value = jax.nn.sigmoid(query_gate[:, width:]).astype(jnp.bfloat16)
    return (normed, query_rows, gate_value)


def on_device(
    n_aa,
    n_ba,
    atom_cond,
    noisy_pos,
    noise_level,
    atom_token,
    token_cond,
    pair,
    pair_bias_weight,
    gains,
    w_pos,
    w_atom_token,
    w_query_gate,
    w_key_value,
    w_attn_out,
    w_up,
    w_down,
    w_token_atom,
    w_pos_out,
):
    tok_rows = token_cond.shape[0]
    block_cols = pair.shape[1]
    head_dim = D // HEADS
    row_index = lax.axis_index("aa")
    col_index = lax.axis_index("ba")
    noise_sigma = noise_level[0]
    inv_scale = 1.0 / jnp.sqrt(noise_sigma * noise_sigma + 1.0)
    scaled_pos = noisy_pos * inv_scale
    atom_state = atom_cond + scaled_pos[0][:, None] * w_pos[0]
    atom_state = atom_state + scaled_pos[1][:, None] * w_pos[1]
    atom_state = atom_state + scaled_pos[2][:, None] * w_pos[2]
    rounded_state = atom_state.astype(jnp.bfloat16)
    local_token = atom_token - row_index * tok_rows
    one_hot = (local_token[:, None] == jnp.arange(tok_rows, dtype=jnp.int32)[None, :]).astype(
        jnp.bfloat16
    )
    group_state, group_ids = exchange(
        [rounded_state, local_token.reshape(1, -1)], "ba", n_ba, False, 0
    )
    group_state = group_state.reshape(-1, group_state.shape[-1])
    summed, counts = token_sums(
        group_ids.reshape(-1), group_state, w_atom_token, tok_rows
    )
    tokens_start = token_cond + summed / counts[:, None]
    normed, query_rows, gate_value = project_start(tokens_start, gains, w_query_gate)
    offset_row = col_index * block_cols % tok_rows
    slice_rows = lax.dynamic_slice_in_dim(normed, offset_row, block_cols, 0)
    block_rows = spread(slice_rows, n_aa, tok_rows, block_cols, 1)
    key_value = jnp.dot(block_rows, w_key_value, preferred_element_type=jnp.float32).astype(
        jnp.bfloat16
    )
    key_heads = key_value[:, :D].reshape(block_cols, HEADS, head_dim)
    value_heads = key_value[:, D:].reshape(block_cols, HEADS, head_dim)
    query_heads = query_rows.reshape(tok_rows, HEADS, head_dim)
    scores = jnp.einsum(
        "ihd,jhd->hij", query_heads, key_heads, preferred_element_type=jnp.float32
    ) * head_dim ** (-0.5) + jnp.einsum(
        "hc,ijc->hij", pair_bias_weight, pair, preferred_element_type=jnp.float32
    )
    block_max = jnp.max(scores, axis=2)
    weights = jnp.exp(scores - block_max[:, :, None])
    block_total = jnp.sum(weights, axis=2)
    partial_out = jnp.einsum(
        "hij,jhd->ihd",
        weights.astype(jnp.bfloat16),
        value_heads,
        preferred_element_type=jnp.float32,
    ).reshape(tok_rows, D)
    own_rows = tok_rows // n_ba
    stats = jnp.concatenate([block_max, block_total], axis=0).T
    out_all, stats_all = exchange(
        [
            partial_out.astype(jnp.bfloat16).reshape(n_ba, own_rows, D),
            stats.reshape(n_ba, own_rows, 2 * HEADS),
        ],
        "ba",
        n_ba,
        True,
        2,
    )
    max_all, total_all = stats_all[:, :, :HEADS], stats_all[:, :, HEADS:]
    factor = jnp.exp(max_all - jnp.max(max_all, axis=0, keepdims=True))
    share = factor / jnp.sum(factor * total_all, axis=0, keepdims=True)
    wide_share = jnp.repeat(share, head_dim, axis=2)
    attended = jnp.sum(wide_share * out_all.astype(jnp.float32), axis=0)
    gate_rows = lax.dynamic_slice_in_dim(gate_value, col_index * own_rows, own_rows, 0)
    mixed_rows = (attended * gate_rows.astype(jnp.float32)).astype(jnp.bfloat16)
    mixed_heads = exchange([mixed_rows], "ba", n_ba, False, 3)[0].reshape(tok_rows, D)
    tokens_mid = tokens_start + jnp.dot(mixed_heads, w_attn_out, preferred_element_type=jnp.float32)
    normed_mid = layer_norm(tokens_mid, gains[1]).astype(jnp.bfloat16)
    gate_up = jnp.dot(normed_mid, w_up, preferred_element_type=jnp.float32)
    hidden_units = w_down.shape[0]
    inner_units = (jax.nn.silu(gate_up[:, :hidden_units]) * gate_up[:, hidden_units:]).astype(
        jnp.bfloat16
    )
    token_out = tokens_mid + jnp.dot(inner_units, w_down, preferred_element_type=jnp.float32)
    normed_out = layer_norm(token_out, gains[2]).astype(jnp.bfloat16)
    token_atom = jnp.dot(normed_out, w_token_atom, preferred_element_type=jnp.float32).astype(
        jnp.bfloat16
    )
    picked = jnp.dot(one_hot, token_atom, preferred_element_type=jnp.float32)
    atom_final = atom_state + picked
    atom_normed = layer_norm(atom_final, 1.0).astype(jnp.bfloat16)
    update = lax.dot_general(
        w_pos_out, atom_normed, (((1,), (1,)), ((), ())), preferred_element_type=jnp.float32
    )
    denoised = noisy_pos * (inv_scale * inv_scale) + update * (noise_sigma * inv_scale)
    return (denoised, token_out)


def solution(mesh):
    in_specs = (
        P(("aa", "ba"), None),
        P(None, ("aa", "ba")),
        P(),
        P(("aa", "ba")),
        P("aa", None),
        P("aa", "ba", None),
        P(),
        P(),
        P(),
        P(),
        P(),
        P(),
        P(),
        P(),
        P(),
        P(),
        P(),
    )
    out_specs = (P(None, ("aa", "ba")), P("aa", None))
    return jax.shard_map(
        functools.partial(on_device, mesh.shape["aa"], mesh.shape["ba"]),
        mesh=mesh, in_specs=in_specs, out_specs=out_specs, check_vma=False
    )
```

profile of v0, /device:TPU:0, one launch (start us, length us, event | category | flops | bytes accessed | tf_op | source)
XLA Modules:
  0.0 120.0 jit_solution(16315514768770571278)
XLA Ops:
  3.5 1.8 %fusion.25.refs_0_ = bf16[384,128]{1,0:T(8,128)(2,1)} fusion(f32[384,128]{1,0:T(8,128)} %param.17, f32[128]{0:T(128)S(1)} %get-tuple-element.19, f32[384]{0:T(512)S(1)} %get-tuple-element.14, f32[128]{0:T(128)S(1)} %get-tuple-element.20, f32[384]{0:T(512)S(1)} %get-tuple-element.15, f32[128]{0:T(128)S(1)} %get-tuple-element.18, f32[384]{0:T(512)S(1)} %get-tuple-element.13), kind=kLoop, calls=%fused_computation.47 | loop fusion | flops 344064 | bytes 301056 | tf_op jit(solution)/shard_map/convert_element_type | solution.py:175
  7.1 13.6 %shard_map.176 = (bf16[8,384,128]{2,1,0:T(8,128)(2,1)}, s32[8,1,384]{2,1,0:T(1,128)}) custom-call(bf16[384,128]{1,0:T(8,128)(2,1)} %fusion.25.refs_0_, s32[1,384]{1,0:T(1,128)} %reshape.89.refs_1_), custom_call_target="tpu_custom_call" | custom-call | tf_op jit(solution)/shard_map/pallas_call | solution.py:51
  20.7 1.1 convert_reduce_fusion
  21.8 4.1 %fusion.38 = (f32[256]{0:T(256)S(1)}, f32[256,768]{1,0:T(8,128)S(1)}) fusion(f32[256,768]{1,0:T(8,128)} %param.21, f32[256]{0:T(256)S(1)} %convert_reduce_fusion, bf16[3072,128]{1,0:T(8,128)(2,1)} %bitcast.53, bf16[128,768]{1,0:T(8,128)(2,1)} %param.26, s32[3072]{0:T(1024)} %bitcast.52), kind=kOutput, calls=%fused_computation.84 | convolution fusion | flops 1818033920 | bytes 2570240 | tf_op jit(solution)/shard_map/dot_general | solution.py:128
  27.7 17.6 %shard_map.177 = bf16[128,768]{1,0:T(8,128)(2,1)} custom-call(bf16[128,768]{1,0:T(8,128)(2,1)} %constant_dynamic-slice_fusion.in_ref), custom_call_target="tpu_custom_call" | custom-call | tf_op jit(solution)/shard_map/pallas_call | solution.py:100
  45.3 2.3 %convolution_convert_fusion = bf16[128,1536]{1,0:T(8,128)(2,1)S(1)} fusion(bf16[128,768]{1,0:T(8,128)(2,1)} %shard_map.177, bf16[768,1536]{1,0:T(8,128)(2,1)} %param.28), kind=kOutput, calls=%fused_computation.5 | convolution fusion | flops 302186496 | bytes 2949120 | tf_op jit(solution)/shard_map/dot_general | solution.py:192
  48.4 1.7 %copy.43 = bf16[128,768]{0,1:T(8,128)(2,1)} copy(bf16[128,768]{1,0:T(8,128)(2,1)} %get-tuple-element.17) | data formatting | bytes 393216 | tf_op jit(solution)/shard_map/slice | solution.py:196
  50.1 7.0 %fusion.33 = f32[16,256,128]{2,0,1:T(8,128)} fusion(bf16[256,128,128]{2,1,0:T(8,128)(2,1)} %param.22, bf16[16,128]{1,0:T(8,128)(2,1)S(1)} %copy-done.14), kind=kOutput, calls=%fused_computation.59 | convolution fusion | flops 134217728 | bytes 10489856 | tf_op jit(solution)/shard_map/hc,ijc->hij/dot_general | solution.py:200
  57.1 3.0 %copy.46 = f32[16,256,128]{1,2,0:T(8,128)} copy(f32[16,256,128]{2,0,1:T(8,128)} %fusion.33) | data formatting | bytes 4194304 | tf_op jit(solution)/shard_map/hc,ijc->hij/dot_general | solution.py:200
  60.8 1.1 copy-done.2
  62.8 1.2 copy.44
  63.9 1.7 %copy.45 = bf16[128,768]{0,1:T(8,128)(2,1)} copy(bf16[128,768]{1,0:T(8,128)(2,1)} %get-tuple-element.16) | data formatting | bytes 393216 | tf_op jit(solution)/shard_map/slice | solution.py:195
  65.7 2.3 %fusion.39 = (f32[16,256]{1,0:T(8,128)S(1)}, f32[16,256,128]{1,2,0:T(8,128)S(1)}) fusion(f32[16,256,128]{1,2,0:T(8,128)} %copy.46, bf16[256,16,48]{0,2,1:T(8,128)(2,1)S(1)} %bitcast.46, bf16[128,16,48]{0,2,1:T(8,128)(2,1)} %bitcast.48), kind=kOutput, calls=%fused_computation.85 | convolution fusion | flops 51900416 | bytes 4800512 | tf_op jit(solution)/shard_map/ihd,jhd->hij/dot_general | solution.py:198
  67.9 1.3 %copy-done.1 = f32[16,256,128]{1,2,0:T(8,128)} copy-done((f32[16,256,128]{1,2,0:T(8,128)}, f32[16,256,128]{1,2,0:T(8,128)S(1)}, u32[]{:S(2)}) %copy-start.1) | copy-done | bytes 2097176
  69.8 1.8 %copy.48 = bf16[256,16,48]{2,1,0:T(8,128)(2,1)} copy(bf16[256,16,48]{0,2,1:T(8,128)(2,1)S(1)} %fusion.6) | data formatting | bytes 786432 | tf_op jit(solution)/shard_map/convert_element_type | solution.py:216
  71.6 2.9 %convert_element_type.69.refs_0_ = bf16[8,32,768]{2,1,0:T(8,128)(2,1)} reshape(bf16[256,16,48]{2,1,0:T(8,128)(2,1)} %copy.48) | data formatting | bytes 786432 | tf_op jit(solution)/shard_map/convert_element_type | solution.py:216
  74.5 1.9 %fusion.2 = f32[16,256]{1,0:T(8,128)S(1)} fusion(f32[16,256,128]{1,2,0:T(8,128)} %copy-done.1, f32[16,256]{1,0:T(8,128)S(1)} %get-tuple-element.23), kind=kLoop, calls=%fused_computation.8 | loop fusion | flops 1044480 | bytes 2129920 | tf_op jit(solution)/shard_map/reduce_sum | solution.py:205
  77.2 8.4 %shard_map.178 = (bf16[8,32,768]{2,1,0:T(8,128)(2,1)}, f32[8,32,32]{2,1,0:T(8,128)}) custom-call(bf16[8,32,768]{2,1,0:T(8,128)(2,1)} %convert_element_type.69.refs_0_, f32[8,32,32]{2,1,0:T(8,128)} %bitcast.50), custom_call_target="tpu_custom_call" | custom-call | tf_op jit(solution)/shard_map/pallas_call | solution.py:51
  85.6 0.9 slice_reduce_fusion
  86.5 1.1 multiply_reduce_fusion.5
  87.6 0.9 fusion.26
  88.5 2.0 %broadcast_in_dim.2 = f32[8,32,16,48]{3,2,1,0:T(8,128)} broadcast(f32[8,32,16]{2,1,0:T(8,128)S(1)} %fusion.26), dimensions={0,1,2} | broadcast | bytes 802816 | tf_op jit(solution)/shard_map/broadcast_in_dim | solution.py:227
  90.5 3.0 %reshape.95 = f32[8,32,768]{2,1,0:T(8,128)} reshape(f32[8,32,16,48]{3,2,1,0:T(8,128)} %broadcast_in_dim.2) | data formatting | bytes 1572864 | tf_op jit(solution)/shard_map/reshape | solution.py:227
  93.5 1.3 %multiply_reduce_fusion.2 = f32[32,768]{1,0:T(8,128)S(1)} fusion(f32[8,32,768]{2,1,0:T(8,128)} %reshape.95, bf16[8,32,768]{2,1,0:T(8,128)(2,1)} %get-tuple-element.9), kind=kLoop, calls=%fused_computation.30 | loop fusion | flops 565248 | bytes 1277952 | tf_op jit(solution)/shard_map/reduce_sum | solution.py:228
  94.8 2.1 %slice.75 = f32[256,768]{1,0:T(8,128)} slice(f32[256,1536]{1,0:T(8,128)} %copy-done.2), slice={[0:256], [768:1536]} | slice | bytes 1572864 | tf_op jit(solution)/shard_map/slice | solution.py:139
  96.9 1.5 %multiply_convert_fusion.8.refs_0_ = bf16[32,768]{1,0:T(8,128)(2,1)} fusion(f32[32,768]{1,0:T(8,128)S(1)} %multiply_reduce_fusion.2, f32[256,768]{1,0:T(8,128)} %slice.75, s32[]{:T(128)S(6)} %select_n.15), kind=kLoop, calls=%fused_computation.56 | loop fusion | flops 172032 | bytes 245764 | tf_op jit(solution)/shard_map/convert_element_type | solution.py:230
  98.4 8.3 %shard_map.179 = bf16[8,32,768]{2,1,0:T(8,128)(2,1)} custom-call(bf16[32,768]{1,0:T(8,128)(2,1)} %multiply_convert_fusion.8.refs_0_), custom_call_target="tpu_custom_call" | custom-call | tf_op jit(solution)/shard_map/pallas_call | solution.py:51
  106.8 2.0 %fusion.40 = (f32[256]{0:T(256)S(1)}, f32[256,768]{1,0:T(8,128)S(1)}) fusion(f32[256,768]{1,0:T(8,128)S(1)} %get-tuple-element.22, bf16[256,768]{1,0:T(8,128)(2,1)} %bitcast.47, bf16[768,768]{1,0:T(8,128)(2,1)} %param.29), kind=kOutput, calls=%fused_computation.86 | convolution fusion | flops 302382848 | bytes 3146752 | tf_op jit(solution)/shard_map/dot_general | solution.py:232
  109.0 4.0 %fusion.14 = f32[256,3072]{1,0:T(8,128)S(1)} fusion(bf16[768,3072]{1,0:T(8,128)(2,1)} %param.30, f32[256,768]{1,0:T(8,128)S(1)} %get-tuple-element.26, f32[768]{0:T(1024)S(1)} %copy-done.16, f32[256]{0:T(256)S(1)} %add_rsqrt_fusion.2, f32[256]{0:T(256)S(1)} %broadcast_multiply_fusion.3), kind=kOutput, calls=%fused_computation.33 | convolution fusion | flops 1208745984 | bytes 8655872 | tf_op jit(solution)/shard_map/dot_general | solution.py:234
  113.0 1.1 fusion.41
  115.3 2.2 %fusion.42 = (f32[384]{0:T(512)}, f32[384,128]{1,0:T(8,128)S(1)}) fusion(bf16[768,128]{1,0:T(8,128)(2,1)} %param.32, f32[256,768]{1,0:T(8,128)S(1)} %get-tuple-element.28, f32[768]{0:T(1024)} %get-tuple-element.10, f32[256]{0:T(256)} %add_rsqrt_fusion.1, f32[256]{0:T(256)} %copy-done.15, s32[384]{0:T(512)} %copy-done.12, f32[128]{0:T(128)} %copy-done.18, ...), kind=kOutput, calls=%fused_computation.88 | convolution fusion | flops 76807808 | bytes 1390592 | tf_op jit(solution)/shard_map/dot_general | solution.py:244
  118.5 1.6 %fusion.10 = f32[3,384]{1,0:T(4,128)} fusion(bf16[3,128]{1,0:T(4,128)(2,1)} %param.33, f32[384,128]{1,0:T(8,128)S(1)} %get-tuple-element.30, f32[384]{0:T(512)S(1)} %add_rsqrt_fusion, f32[384]{0:T(512)S(1)} %broadcast_multiply_fusion.1, f32[3,384]{1,0:T(4,128)S(1)} %copy-done.6, f32[]{:T(128)S(6)} %mul.238, f32[]{:T(128)S(6)} %mul.187), kind=kOutput, calls=%fused_computation.23 | convolution fusion | flops 445824 | bytes 209672 | tf_op jit(solution)/shard_map/dot_general | solution.py:247
  (66 shorter events, 11.7 us)
Async XLA Ops:
  0.6 59.4 %copy-start = (bf16[768,1536]{1,0:T(8,128)(2,1)S(1)}, bf16[768,1536]{1,0:T(8,128)(2,1)}, u32[]{:S(2)}) copy-start(bf16[768,1536]{1,0:T(8,128)(2,1)} %param.27) | copy-start | bytes 7077892
  1.5 20.3 %copy-start.17 = (f32[128]{0:T(128)}, f32[128]{0:T(128)S(1)}, u32[]{:S(2)}) copy-start(f32[128]{0:T(128)S(1)} %get-tuple-element.18) | copy-start | bytes 1540
  1.5 20.3 %copy-start.18 = (f32[128]{0:T(128)}, f32[128]{0:T(128)S(1)}, u32[]{:S(2)}) copy-start(f32[128]{0:T(128)S(1)} %get-tuple-element.19) | copy-start | bytes 1540
  1.5 20.3 %copy-start.19 = (f32[128]{0:T(128)}, f32[128]{0:T(128)S(1)}, u32[]{:S(2)}) copy-start(f32[128]{0:T(128)S(1)} %get-tuple-element.20) | copy-start | bytes 1540
  2.9 0.6 copy-start.7
  2.9 2.3 %copy-start.9 = (f32[384]{0:T(512)}, f32[384]{0:T(512)S(1)}, u32[]{:S(2)}) copy-start(f32[384]{0:T(512)S(1)} %get-tuple-element.14) | copy-start | bytes 4612
  3.0 2.3 %copy-start.11 = (f32[384]{0:T(512)}, f32[384]{0:T(512)S(1)}, u32[]{:S(2)}) copy-start(f32[384]{0:T(512)S(1)} %get-tuple-element.15) | copy-start | bytes 4612
  6.0 0.6 copy-start.12
  21.8 4.1 %copy-start.13 = (f32[3,768]{1,0:T(4,128)S(1)}, f32[3,768]{1,0:T(4,128)}, u32[]{:S(2)}) copy-start(f32[3,768]{1,0:T(4,128)} %param.24) | copy-start | bytes 27652
  45.3 4.8 %copy-start.14 = (bf16[16,128]{1,0:T(8,128)(2,1)S(1)}, bf16[16,128]{1,0:T(8,128)(2,1)}, u32[]{:S(2)}) copy-start(bf16[16,128]{1,0:T(8,128)(2,1)} %param.23) | copy-start | bytes 12292
  60.8 1.2 copy-start.2
  65.7 3.6 %copy-start.4 = (bf16[128,768]{0,1:T(8,128)(2,1)S(1)}, bf16[128,768]{0,1:T(8,128)(2,1)}, u32[]{:S(2)}) copy-start(bf16[128,768]{0,1:T(8,128)(2,1)} %copy.43) | copy-start | bytes 589828
  67.9 1.4 %copy-start.1 = (f32[16,256,128]{1,2,0:T(8,128)}, f32[16,256,128]{1,2,0:T(8,128)S(1)}, u32[]{:S(2)}) copy-start(f32[16,256,128]{1,2,0:T(8,128)S(1)} %get-tuple-element.24) | copy-start | bytes 6291460
  98.4 10.6 %copy-start.16 = (f32[768]{0:T(1024)S(1)}, f32[768]{0:T(1024)}, u32[]{:S(2)}) copy-start(f32[768]{0:T(1024)} %get-tuple-element.12) | copy-start | bytes 9220
  109.0 4.0 %copy-start.20 = (bf16[1536,768]{1,0:T(8,128)(2,1)S(1)}, bf16[1536,768]{1,0:T(8,128)(2,1)}, u32[]{:S(2)}) copy-start(bf16[1536,768]{1,0:T(8,128)(2,1)} %param.31) | copy-start | bytes 7077892
  113.0 2.3 %copy-start.5 = (f32[384,128]{1,0:T(8,128)S(1)}, f32[384,128]{1,0:T(8,128)}, u32[]{:S(2)}) copy-start(f32[384,128]{1,0:T(8,128)} %param.17) | copy-start | bytes 589828
  113.0 2.3 %copy-start.8 = (f32[384]{0:T(512)S(1)}, f32[384]{0:T(512)}, u32[]{:S(2)}) copy-start(f32[384]{0:T(512)} %copy-done.7) | copy-start | bytes 4612
  113.0 2.3 %copy-start.10 = (f32[384]{0:T(512)S(1)}, f32[384]{0:T(512)}, u32[]{:S(2)}) copy-start(f32[384]{0:T(512)} %copy-done.9) | copy-start | bytes 4612
  114.1 5.9 %copy-start.3 = (f32[256,768]{1,0:T(8,128)}, f32[256,768]{1,0:T(8,128)S(1)}, u32[]{:S(2)}) copy-start(f32[256,768]{1,0:T(8,128)S(1)} %get-tuple-element.28) | copy-start | bytes 2359300
  114.1 4.4 %copy-start.6 = (f32[3,384]{1,0:T(4,128)S(1)}, f32[3,384]{1,0:T(4,128)}, u32[]{:S(2)}) copy-start(f32[3,384]{1,0:T(4,128)} %param.18) | copy-start | bytes 13828
  114.1 0.6 copy-start.15
where the time goes:
time: 121 us; the launch traced here: 120 us
  Pallas kernels  47.9 us (40%)
  local copies, waits for them, and re-layouts  28.5 us (24%)
  matrix products  27.6 us (23%)
  other arithmetic  14.4 us (12%)
  between operations  1.66 us (1%)
    pallas_call x3, Pallas kernels, exchange(): pl.pallas_call(kernel, out_shape=[jax.ShapeDtypeStruct(s, x.dtype) for s,...  30.3 us
    pallas_call x1, Pallas kernels, spread(): pl.pallas_call(kernel, out_shape=jax.ShapeDtypeStruct(rows.shape, rows.dt...  17.6 us
    dot_general x1, matrix products, on_device(): jnp.einsum('hc,ijc->hij', pair_bias_weight, pair, preferred_element_type=...  6.97 us
    convert_element_type x2, local copies, waits for them, and re-layouts, on_device(): partial_out.astype(jnp.bfloat16).reshape(n_ba, own_rows, D)  4.72 us
    dot_general x1, matrix products, token_sums(): lax.dot_general(selector, hidden_atom, (((1,), (0,)), ((), ())), preferre...  4.12 us
    unnamed x42, local copies, waits for them, and re-layouts  4.06 us
    dot_general x1, matrix products, on_device(): gate_up = jnp.dot(normed_mid, w_up, preferred_element_type=jnp.float32)  3.95 us
    reshape x1, local copies, waits for them, and re-layouts, on_device(): wide_share = jnp.repeat(share, head_dim, axis=2)  3.03 us

commit v1 on v0

v1 whole, which is shorter than its diff:
```python
import functools

import jax
import jax.numpy as jnp
from jax import lax
from jax.experimental import pallas as pl
from jax.experimental.pallas import tpu as pltpu
from jax.sharding import PartitionSpec as P

MESH = pl.DeviceIdType.MESH
F32 = jnp.float32
BF16 = jnp.bfloat16
LANES = 128
PAIR_CHUNKS = 8
EARLY_CHUNKS = 4
BIAS_ROWS = 8
TILE = 256


def flip(index, mask):
    out = index
    bit = 1
    while bit <= mask:
        if mask & bit:
            out = out + bit - 2 * bit * lax.rem(index // bit, 2)
        bit *= 2
    return out


def far_first(count):
    return sorted(range(1, count), key=lambda m: (-bin(m).count("1"), m))


def norm(values, gain_row):
    mean_value = jnp.mean(values, axis=-1, keepdims=True)
    centered = values - mean_value
    variance = jnp.mean(centered * centered, axis=-1, keepdims=True)
    scaled = centered * lax.rsqrt(variance + 1e-05)
    return scaled if gain_row is None else scaled * gain_row


def dot(a, b):
    return jnp.dot(a, b, preferred_element_type=F32)


def dot_nt(a, b):
    return lax.dot_general(a, b, (((1,), (1,)), ((), ())), preferred_element_type=F32)


def step_kernel(
    n_aa,
    n_ba,
    atom_hbm,
    noisy_ref,
    noise_ref,
    ids_ref,
    tok_hbm,
    pair_hbm,
    bias_w_ref,
    gains_ref,
    w_pos_ref,
    wat_hbm,
    wqg_hbm,
    wkv_hbm,
    wo_hbm,
    wup_hbm,
    wdn_hbm,
    wta_hbm,
    w_pos_out_ref,
    den_ref,
    tok_out_hbm,
    v_state,
    v_post,
    v_onehot,
    v_tok,
    v_pair,
    v_bias,
    v_wat,
    v_wqg,
    v_wkv,
    v_wo,
    v_wup,
    v_wdn,
    v_wta,
    ids_all,
    sum_send,
    sum_recv,
    rows_own,
    rows_z,
    rows_kv,
    q_own,
    q_all,
    v_km,
    v_vm,
    v_p,
    o_send,
    o_recv,
    st_send,
    st_recv,
    v_inner,
    t_own,
    t_all,
    ta_own,
    ta_all,
    load_sem,
    pair_sem,
    ids_sems,
    sum_sems,
    z_sems,
    kv_send,
    kv_recv,
    kv_local,
    q_sems,
    o_sems,
    st_sems,
    t_sems,
    ta_sems,
    out_sem,
):
    atoms = ids_ref.shape[1]
    atoms_pad = v_state.shape[0]
    tok_rows, cols, channels = v_pair.shape
    heads = bias_w_ref.shape[0]
    own, width = v_tok.shape
    head_dim = width // heads
    hidden = v_wdn.shape[0]
    per = tok_rows // cols
    pieces = cols // own
    me_a = lax.axis_index("aa")
    me_b = lax.axis_index("ba")

    barrier = pltpu.get_barrier_semaphore()
    for x in range(1, n_ba):
        pl.semaphore_signal(barrier, inc=1, device_id={"ba": flip(me_b, x)}, device_id_type=MESH)
    for x in range(1, n_aa):
        pl.semaphore_signal(barrier, inc=1, device_id={"aa": flip(me_a, x)}, device_id_type=MESH)

    own_start = pl.multiple_of(me_b * own, own)
    loads = {}
    for slot, (name, src, dst) in enumerate(
        [
            ("atom", atom_hbm, v_state.at[pl.ds(0, atoms)]),
            ("wat", wat_hbm, v_wat),
            ("tok", tok_hbm.at[pl.ds(own_start, own)], v_tok),
            ("wqg", wqg_hbm, v_wqg),
            ("wkv", wkv_hbm, v_wkv),
            ("wo", wo_hbm, v_wo),
            ("wup", wup_hbm, v_wup),
            ("wdn", wdn_hbm, v_wdn),
            ("wta", wta_hbm, v_wta),
        ]
    ):
        loads[name] = pltpu.make_async_copy(src, dst, load_sem.at[slot])
    step = tok_rows // PAIR_CHUNKS
    pair_loads = [
        pltpu.make_async_copy(
            pair_hbm.at[pl.ds(c * step, step)], v_pair.at[pl.ds(c * step, step)], pair_sem.at[c]
        )
        for c in range(PAIR_CHUNKS)
    ]
    for name in ("atom", "wat", "tok", "wqg"):
        loads[name].start()
    for copy in pair_loads:
        copy.start()
    for name in ("wkv", "wo", "wup", "wdn", "wta"):
        loads[name].start()

    def ba_copy(src, dst, sems, x):
        return pltpu.make_async_remote_copy(
            src_ref=src,
            dst_ref=dst,
            send_sem=sems.at[0, x - 1],
            recv_sem=sems.at[1, x - 1],
            device_id={"ba": flip(me_b, x)},
            device_id_type=MESH,
        )

    order = far_first(n_ba)

    sigma = jnp.full((3, atoms), noise_ref[0], F32)
    inv_scale = 1.0 / jnp.sqrt(sigma * sigma + 1.0)
    local_ids = ids_ref[...] - me_a * tok_rows
    v_post[...] = jnp.full(v_post.shape, -1.0, F32)
    v_post[0:3, 0:atoms] = noisy_ref[...] * inv_scale
    v_post[3:4, 0:atoms] = local_ids.astype(F32)
    ids_row = v_post[3:4, :]
    columns = v_post[...].T
    if atoms_pad > atoms:
        v_state[pl.ds(atoms, atoms_pad - atoms), :] = jnp.zeros(
            (atoms_pad - atoms, channels), F32
        )
    loads["atom"].wait()
    state = v_state[...]
    for c in range(3):
        state = state + columns[:, c : c + 1] * w_pos_ref[c : c + 1, :]
    v_state[...] = state
    lane_id = lax.broadcasted_iota(jnp.int32, (atoms_pad, tok_rows), 1).astype(F32)
    v_onehot[...] = jnp.where(columns[:, 3:4] == lane_id, 1.0, 0.0).astype(BF16)
    row_id = lax.broadcasted_iota(jnp.int32, (tok_rows, atoms_pad), 0).astype(F32)
    selector = jnp.where(row_id == ids_row, 1.0, 0.0).astype(BF16)
    loads["wat"].wait()
    hidden_atom = jnp.maximum(dot(state.astype(BF16), v_wat[...]), 0.0).astype(BF16)
    partial_sums = dot(selector, hidden_atom).astype(BF16)
    sum_send[...] = partial_sums.reshape(n_ba, own, width)

    pl.semaphore_wait(barrier, n_ba - 1 + n_aa - 1)
    ids_copies = {x: ba_copy(ids_ref, ids_all.at[x - 1], ids_sems, x) for x in order}
    sum_copies = {
        x: ba_copy(sum_send.at[flip(me_b, x)], sum_recv.at[x - 1], sum_sems, x) for x in order
    }
    for x in order:
        ids_copies[x].start()
        sum_copies[x].start()

    bias_w = bias_w_ref[...]

    def bias_chunk(c):
        pair_loads[c].wait()

        def rows(r, carry):
            start = c * step + r * BIAS_ROWS
            block = v_pair[pl.ds(start, BIAS_ROWS)].reshape(BIAS_ROWS * cols, channels)
            out = dot_nt(bias_w, block)
            for i in range(BIAS_ROWS):
                where = pl.multiple_of((start + i) * heads, heads)
                v_bias[pl.ds(where, heads), :] = out[:, i * cols : (i + 1) * cols]
            return carry

        lax.fori_loop(0, step // BIAS_ROWS, rows, 0)

    for c in range(EARLY_CHUNKS):
        bias_chunk(c)

    first_row = me_a * tok_rows + me_b * own
    own_row = lax.broadcasted_iota(jnp.int32, (own, atoms), 0) + first_row
    hits = jnp.where(own_row == ids_ref[...], 1.0, 0.0)
    summed = sum_send[me_b].astype(F32)
    for x in order:
        ids_copies[x].wait_recv()
        hits = hits + jnp.where(own_row == ids_all[x - 1], 1.0, 0.0)
    counts = jnp.sum(hits, axis=1, keepdims=True)
    for x in order:
        sum_copies[x].wait_recv()
        summed = summed + sum_recv[x - 1].astype(F32)
    loads["tok"].wait()
    tokens_start = v_tok[...] + summed / counts
    v_tok[...] = tokens_start
    normed = norm(tokens_start, gains_ref[0:1, :]).astype(BF16)
    rows_own[...] = normed

    z_order = far_first(n_aa)
    z_copies = {
        x: pltpu.make_async_remote_copy(
            src_ref=rows_own,
            dst_ref=rows_z.at[x - 1],
            send_sem=z_sems.at[0, x - 1],
            recv_sem=z_sems.at[1, x - 1],
            device_id={"aa": flip(me_a, x)},
            device_id_type=MESH,
        )
        for x in z_order
    }
    for x in z_order:
        z_copies[x].start()

    def forward(x):
        src = rows_own if x == 0 else rows_z.at[x - 1]
        group = flip(me_a, x)
        target = group * per + me_b // pieces
        dst = rows_kv.at[lax.rem(me_b, pieces)]
        remote = pltpu.make_async_remote_copy(
            src_ref=src,
            dst_ref=dst,
            send_sem=kv_send.at[x],
            recv_sem=kv_recv.at[lax.rem(me_b, pieces)],
            device_id={"ba": target},
            device_id_type=MESH,
        )
        local = pltpu.make_async_copy(src, dst, kv_local)
        return target, remote, local

    def start_forward(x):
        target, remote, local = forward(x)

        @pl.when(target != me_b)
        def _():
            remote.start()

        @pl.when(target == me_b)
        def _():
            local.start()

    start_forward(0)
    loads["wqg"].wait()
    query = dot(normed, v_wqg[:, 0:width]).astype(BF16)
    q_own[...] = query
    q_all[me_b] = query
    q_copies = {x: ba_copy(q_own, q_all.at[me_b], q_sems, x) for x in order}
    for x in order:
        q_copies[x].start()
    gate = jax.nn.sigmoid(dot(normed, v_wqg[:, width : 2 * width])).astype(BF16)

    for c in range(EARLY_CHUNKS, PAIR_CHUNKS):
        bias_chunk(c)
    for x in reversed(z_order):
        z_copies[x].wait_recv()
        start_forward(x)
    loads["wkv"].wait()
    for s in range(pieces):
        source = pieces * lax.rem(me_b, per) + s

        @pl.when(source == me_b)
        def _():
            pltpu.make_async_copy(rows_own, rows_kv.at[s], kv_local).wait()

        @pl.when(source != me_b)
        def _():
            pltpu.make_async_remote_copy(
                src_ref=rows_own,
                dst_ref=rows_kv.at[s],
                send_sem=kv_send.at[0],
                recv_sem=kv_recv.at[s],
                device_id={"ba": source},
                device_id_type=MESH,
            ).wait_recv()

    key_value = dot(rows_kv[...].reshape(cols, width), v_wkv[...]).astype(BF16)
    keys, values = key_value[:, :width], key_value[:, width:]
    spans = []
    for h in range(heads):
        lo = h * head_dim // LANES * LANES
        hi = ((h + 1) * head_dim + LANES - 1) // LANES * LANES
        spans.append((lo, hi))
        lane = lax.broadcasted_iota(jnp.int32, (cols, hi - lo), 1) + lo
        mine = (lane >= h * head_dim) & (lane < (h + 1) * head_dim)
        v_km[h, :, 0 : hi - lo] = jnp.where(mine, keys[:, lo:hi].astype(F32), 0.0).astype(BF16)
    tiles = []
    for t in range(width // TILE):
        h0 = t * TILE // head_dim
        h1 = (t * TILE + TILE - 1) // head_dim
        tiles.append((h0, h1))
        part = values[:, t * TILE : (t + 1) * TILE].astype(F32)
        lane = lax.broadcasted_iota(jnp.int32, (cols, TILE), 1) + t * TILE
        for h in range(h0, h1 + 1):
            mine = (lane >= h * head_dim) & (lane < (h + 1) * head_dim)
            v_vm[t, (h - h0) * cols : (h - h0 + 1) * cols, :] = jnp.where(mine, part, 0.0).astype(
                BF16
            )

    for x in order:
        q_copies[x].wait_recv()

    scale = head_dim ** (-0.5)
    rows2 = 2 * own
    lane = lax.broadcasted_iota(jnp.int32, (rows2, LANES), 1)
    groups = own // 8
    o_copies = {x: ba_copy(o_send.at[flip(me_b, x)], o_recv.at[x - 1], o_sems, x) for x in order}
    st_copies = {
        x: ba_copy(st_send.at[flip(me_b, x)], st_recv.at[x - 1], st_sems, x) for x in order
    }
    for d in far_first(n_ba // 2) + [0]:
        duo = flip(me_b // 2, d)
        stats = jnp.zeros((rows2, LANES), F32)
        q_rows = q_all[pl.ds(2 * duo, 2)].reshape(rows2, width)
        for h in range(heads):
            lo, hi = spans[h]
            scores = dot_nt(q_rows[:, lo:hi], v_km[h, :, 0 : hi - lo]) * scale
            scores = scores + v_bias[pl.ds(duo * (rows2 * heads) + h, rows2, stride=heads), :]
            top = jnp.max(scores, axis=1, keepdims=True)
            weights = jnp.exp(scores - top)
            total = jnp.sum(weights, axis=1, keepdims=True)
            stats = jnp.where(lane == h, top, stats)
            stats = jnp.where(lane == heads + h, total, stats)
            v_p[:, h * cols : (h + 1) * cols] = weights.astype(BF16)
        for t, (h0, h1) in enumerate(tiles):
            out = dot(
                v_p[:, h0 * cols : (h1 + 1) * cols], v_vm[t, 0 : (h1 - h0 + 1) * cols, :]
            )
            o_send[pl.ds(2 * duo, 2), :, t * TILE : (t + 1) * TILE] = out.astype(BF16).reshape(
                2, own, TILE
            )
        for c in range(2):
            packed = stats[c * own : c * own + 8]
            for g in range(1, groups):
                piece = pltpu.roll(stats[c * own + 8 * g : c * own + 8 * g + 8], 2 * heads * g, 1)
                packed = jnp.where(lane[0:8] >= 2 * heads * g, piece, packed)
            st_send[2 * duo + c] = packed
        for x in (2 * d + 1, 2 * d):
            if x:
                st_copies[x].start()
                o_copies[x].start()

    def unpack(packed):
        parts = [packed]
        for g in range(1, groups):
            parts.append(pltpu.roll(packed, LANES - 2 * heads * g, 1))
        return jnp.concatenate(parts, axis=0)

    tops = [unpack(st_send[me_b])]
    for x in range(1, n_ba):
        st_copies[x].wait_recv()
        tops.append(unpack(st_recv[x - 1]))
    overall = tops[0]
    for top in tops[1:]:
        overall = jnp.maximum(overall, top)
    factors = [jnp.exp(top - overall) for top in tops]
    denominator = jnp.zeros((own, LANES), F32)
    for factor, top in zip(factors, tops):
        denominator = denominator + factor * pltpu.roll(top, LANES - heads, 1)
    head_row = lax.broadcasted_iota(jnp.int32, (LANES, width), 0)
    head_lane = lax.broadcasted_iota(jnp.int32, (LANES, width), 1)
    inside = (head_lane >= head_row * head_dim) & (head_lane < (head_row + 1) * head_dim)
    spread = jnp.where(inside, 1.0, 0.0).astype(BF16)
    live = lane[0:own] < heads
    shares = jnp.concatenate(
        [jnp.where(live, factor / denominator, 0.0) for factor in factors], axis=0
    )
    coarse = shares.astype(BF16)
    fine = (shares - coarse.astype(F32)).astype(BF16)
    wide = dot(coarse, spread) + dot(fine, spread)
    attended = wide[0:own] * o_send[me_b].astype(F32)
    for x in range(1, n_ba):
        o_copies[x].wait_recv()
        attended = attended + wide[x * own : (x + 1) * own] * o_recv[x - 1].astype(F32)
    mixed = (attended * gate.astype(F32)).astype(BF16)
    loads["wo"].wait()
    tokens_mid = v_tok[...] + dot(mixed, v_wo[...])
    normed_mid = norm(tokens_mid, gains_ref[1:2, :]).astype(BF16)
    loads["wup"].wait()
    part = 512
    for n in range(0, hidden, part):
        first = dot(normed_mid, v_wup[:, n : n + part])
        second = dot(normed_mid, v_wup[:, hidden + n : hidden + n + part])
        v_inner[:, n : n + part] = (first * jax.nn.sigmoid(first) * second).astype(BF16)
    loads["wdn"].wait()
    token_out = tokens_mid + dot(v_inner[...], v_wdn[...])
    token_round = token_out.astype(BF16)
    t_own[...] = token_round
    t_all[me_b] = token_round
    t_copies = {x: ba_copy(t_own, t_all.at[me_b], t_sems, x) for x in order}
    for x in order:
        t_copies[x].start()
    loads["wta"].wait()
    normed_out = norm(token_out, gains_ref[2:3, :]).astype(BF16)
    token_atom = dot(normed_out, v_wta[...]).astype(BF16)
    ta_own[...] = token_atom
    ta_all[me_b] = token_atom
    ta_copies = {x: ba_copy(ta_own, ta_all.at[me_b], ta_sems, x) for x in order}
    for x in order:
        ta_copies[x].start()
    for x in order:
        ta_copies[x].wait_recv()
    picked = dot(v_onehot[...], ta_all[...].reshape(tok_rows, channels))
    atom_normed = norm(v_state[...] + picked, None).astype(BF16)
    update = dot_nt(w_pos_out_ref[...], atom_normed)[:, 0:atoms]
    den_ref[...] = noisy_ref[...] * (inv_scale * inv_scale) + update * (sigma * inv_scale)
    for x in order:
        t_copies[x].wait_recv()
    result = pltpu.make_async_copy(t_all, tok_out_hbm, out_sem)
    result.start()
    for x in order:
        for copies in (ids_copies, sum_copies, q_copies, st_copies, o_copies, t_copies, ta_copies):
            copies[x].wait_send()
    for x in z_order:
        z_copies[x].wait_send()
    for x in range(n_aa):
        target, remote, _ = forward(x)

        @pl.when(target != me_b)
        def _():
            remote.wait_send()

    result.wait()


def on_device(
    n_aa,
    n_ba,
    atom_cond,
    noisy_pos,
    noise_level,
    atom_token,
    token_cond,
    pair,
    pair_bias_weight,
    gains,
    w_pos,
    w_atom_token,
    w_query_gate,
    w_key_value,
    w_attn_out,
    w_up,
    w_down,
    w_token_atom,
    w_pos_out,
):
    atoms, channels = atom_cond.shape
    atoms_pad = -(-atoms // LANES) * LANES
    tok_rows, width = token_cond.shape
    cols = pair.shape[1]
    heads = pair_bias_weight.shape[0]
    own = tok_rows // n_ba
    pieces = cols // own
    head_dim = width // heads
    tile_heads = max(
        (t * TILE + TILE - 1) // head_dim - t * TILE // head_dim + 1 for t in range(width // TILE)
    )
    vmem = pl.BlockSpec(memory_space=pltpu.VMEM)
    smem = pl.BlockSpec(memory_space=pltpu.SMEM)
    hbm = pl.BlockSpec(memory_space=pl.ANY)
    dma = pltpu.SemaphoreType.DMA
    denoised, tokens = pl.pallas_call(
        functools.partial(step_kernel, n_aa, n_ba),
        out_shape=[
            jax.ShapeDtypeStruct((3, atoms), F32),
            jax.ShapeDtypeStruct((n_ba, own, width), BF16),
        ],
        in_specs=[hbm, vmem, smem, vmem, hbm, hbm, vmem, vmem, vmem] + [hbm] * 7 + [vmem],
        out_specs=[vmem, hbm],
        scratch_shapes=[
            pltpu.VMEM((atoms_pad, channels), F32),
            pltpu.VMEM((LANES, atoms_pad), F32),
            pltpu.VMEM((atoms_pad, tok_rows), BF16),
            pltpu.VMEM((own, width), F32),
            pltpu.VMEM(pair.shape, BF16),
            pltpu.VMEM((tok_rows * heads, cols), F32),
            pltpu.VMEM(w_atom_token.shape, BF16),
            pltpu.VMEM(w_query_gate.shape, BF16),
            pltpu.VMEM(w_key_value.shape, BF16),
            pltpu.VMEM(w_attn_out.shape, BF16),
            pltpu.VMEM(w_up.shape, BF16),
            pltpu.VMEM(w_down.shape, BF16),
            pltpu.VMEM(w_token_atom.shape, BF16),
            pltpu.VMEM((n_ba - 1, 1, atoms), jnp.int32),
            pltpu.VMEM((n_ba, own, width), BF16),
            pltpu.VMEM((n_ba - 1, own, width), BF16),
            pltpu.VMEM((own, width), BF16),
            pltpu.VMEM((n_aa - 1, own, width), BF16),
            pltpu.VMEM((pieces, own, width), BF16),
            pltpu.VMEM((own, width), BF16),
            pltpu.VMEM((n_ba, own, width), BF16),
            pltpu.VMEM((heads, cols, 2 * LANES), BF16),
            pltpu.VMEM((width // TILE, tile_heads * cols, TILE), BF16),
            pltpu.VMEM((2 * own, heads * cols), BF16),
            pltpu.VMEM((n_ba, own, width), BF16),
            pltpu.VMEM((n_ba - 1, own, width), BF16),
            pltpu.VMEM((n_ba, 8, LANES), F32),
            pltpu.VMEM((n_ba - 1, 8, LANES), F32),
            pltpu.VMEM((own, w_down.shape[0]), BF16),
            pltpu.VMEM((own, width), BF16),
            pltpu.VMEM((n_ba, own, width), BF16),
            pltpu.VMEM((own, channels), BF16),
            pltpu.VMEM((n_ba, own, channels), BF16),
            dma((9,)),
            dma((PAIR_CHUNKS,)),
            dma((2, n_ba - 1)),
            dma((2, n_ba - 1)),
            dma((2, n_aa - 1)),
            dma((n_aa,)),
            dma((pieces,)),
            dma,
            dma((2, n_ba - 1)),
            dma((2, n_ba - 1)),
            dma((2, n_ba - 1)),
            dma((2, n_ba - 1)),
            dma((2, n_ba - 1)),
            dma,
        ],
        compiler_params=pltpu.CompilerParams(
            collective_id=0, has_side_effects=True, vmem_limit_bytes=56 * 1024 * 1024
        ),
    )(
        atom_cond,
        noisy_pos,
        noise_level,
        atom_token.reshape(1, -1),
        token_cond,
        pair,
        pair_bias_weight,
        gains,
        w_pos,
        w_atom_token,
        w_query_gate,
        w_key_value,
        w_attn_out,
        w_up,
        w_down,
        w_token_atom,
        w_pos_out,
    )
    return denoised, tokens.reshape(tok_rows, width).astype(F32)


def solution(mesh):
    in_specs = (
        P(("aa", "ba"), None),
        P(None, ("aa", "ba")),
        P(),
        P(("aa", "ba")),
        P("aa", None),
        P("aa", "ba", None),
    ) + (P(),) * 11
    out_specs = (P(None, ("aa", "ba")), P("aa", None))
    return jax.shard_map(
        functools.partial(on_device, mesh.shape["aa"], mesh.shape["ba"]),
        mesh=mesh,
        in_specs=in_specs,
        out_specs=out_specs,
        check_vma=False,
    )
```

time: 121 us -> 47.7 us (0.39)
  matrix products: 27.6 us -> 0 us
  local copies, waits for them, and re-layouts: 28.5 us -> 2.53 us
  other arithmetic: 14.4 us -> 1.93 us
  Pallas kernels: 47.9 us -> 41.7 us
    dot_general x11 -> x0, matrix products: 27.6 us -> none  [the longest x1 6.97 us: on_device(): jnp.einsum('hc,ijc->hij', pair_bias_weight, pair, preferred_element_type=...]
    slice x8 -> x0, local copies, waits for them, and re-layouts: 8.91 us -> none  [the longest x2 2.51 us: on_device(): key_heads = key_value[:, :D].reshape(block_cols, HEADS, head_dim)]
    reduce_sum x8 -> x0, other arithmetic: 6.3 us -> none  [the longest x1 1.9 us: on_device(): block_total = jnp.sum(weights, axis=2)]
    pallas_call x4 -> x1, Pallas kernels: 47.9 us -> 41.7 us  [on_device(): pl.pallas_call(functools.partial(step_kernel, n_aa, n_ba), out_shape=[jax...]
    convert_element_type x2 -> x0, local copies, waits for them, and re-layouts: 4.72 us -> none  [on_device(): partial_out.astype(jnp.bfloat16).reshape(n_ba, own_rows, D)]
    dot_general x1 -> x0, local copies, waits for them, and re-layouts: 2.95 us -> none  [on_device(): jnp.einsum('hc,ijc->hij', pair_bias_weight, pair, preferred_element_type=...]
    unnamed x42 -> x1, local copies, waits for them, and re-layouts: 4.06 us -> 1.29 us
    reshape x2 -> x1, local copies, waits for them, and re-layouts: 3.59 us -> 1.25 us  [on_device(): atom_token.reshape(1, -1)]
where the time goes in v1:
time: 47.7 us; the launch traced here: 47.4 us
  Pallas kernels  41.7 us (87%)
  local copies, waits for them, and re-layouts  2.53 us (5%)
  other arithmetic  1.93 us (4%)
  between operations  1.29 us (3%)
    pallas_call x1, Pallas kernels, on_device(): pl.pallas_call(functools.partial(step_kernel, n_aa, n_ba), out_shape=[jax...  41.7 us
    convert_element_type x1, other arithmetic, on_device(): return (denoised, tokens.reshape(tok_rows, width).astype(F32))  1.93 us
    unnamed x1, local copies, waits for them, and re-layouts  1.29 us
    reshape x1, local copies, waits for them, and re-layouts, on_device(): atom_token.reshape(1, -1)  1.25 us

profile of v1, /device:TPU:0, one launch (start us, length us, event | category | flops | bytes accessed | tf_op | source)
XLA Modules:
  0.0 47.4 jit_solution(437574802403051098)
XLA Ops:
  1.3 1.2 %reshape.10.ids_ref = s32[1,384]{1,0:T(1,128)} reshape(s32[384]{0:T(512)} %param.20) | data formatting | bytes 3072 | tf_op jit(solution)/shard_map/reshape | solution.py:576
  2.5 41.7 %shard_map.176 = (f32[3,384]{1,0:T(4,128)}, bf16[8,32,768]{2,1,0:T(8,128)(2,1)}) custom-call(f32[384,128]{1,0:T(8,128)} %atom_hbm.1, f32[3,384]{1,0:T(4,128)} %noisy_ref.1, f32[1]{0:T(128)S(6)} %copy.20.noise_ref, s32[1,384]{1,0:T(1,128)} %reshape.10.ids_ref, f32[256,768]{1,0:T(8,128)} %tok_hbm.1, bf16[256,128,128]{2,1,0:T(8,128)(2,1)} %pair_hbm.1, ...), custom_call_target="tpu_custom_call" | custom-call | tf_op jit(solution)/shard_map/pallas_call | solution.py:512
  44.2 1.9 %bitcast_convert_fusion = f32[256,768]{1,0:T(8,128)} fusion(bf16[8,32,768]{2,1,0:T(8,128)(2,1)} %get-tuple-element.5), kind=kLoop, calls=%fused_computation | loop fusion | flops 196608 | bytes 1179648 | tf_op jit(solution)/shard_map/convert_element_type | solution.py:591
  46.1 1.3 %copy.21 = f32[3,384]{1,0:T(4,128)} copy(f32[3,384]{1,0:T(4,128)} %get-tuple-element.8) | data formatting | bytes 9216

commit v2 on v1

v2 whole, which is shorter than its diff:
```python
import functools

import jax
import jax.numpy as jnp
from jax import lax
from jax.experimental import pallas as pl
from jax.experimental.pallas import tpu as pltpu
from jax.sharding import PartitionSpec as P

MESH = pl.DeviceIdType.MESH
F32 = jnp.float32
BF16 = jnp.bfloat16
LANES = 128
PAIR_CHUNKS = 8
EARLY_CHUNKS = 4
BIAS_ROWS = 8


def flip(index, mask):
    out = index
    bit = 1
    while bit <= mask:
        if mask & bit:
            out = out + bit - 2 * bit * lax.rem(index // bit, 2)
        bit *= 2
    return out


def far_first(count):
    return sorted(range(1, count), key=lambda m: (-bin(m).count("1"), m))


def norm(values, gain_row):
    mean_value = jnp.mean(values, axis=-1, keepdims=True)
    centered = values - mean_value
    variance = jnp.mean(centered * centered, axis=-1, keepdims=True)
    scaled = centered * lax.rsqrt(variance + 1e-05)
    return scaled if gain_row is None else scaled * gain_row


def dot(a, b):
    return jnp.dot(a, b, preferred_element_type=F32)


def dot_nt(a, b):
    return lax.dot_general(a, b, (((1,), (1,)), ((), ())), preferred_element_type=F32)


def step_kernel(
    n_aa,
    n_ba,
    atom_hbm,
    noisy_ref,
    noise_ref,
    ids_hbm,
    tok_hbm,
    pair_hbm,
    bias_w_ref,
    gains_ref,
    w_pos_ref,
    wat_hbm,
    wqg_hbm,
    wkv_hbm,
    wo_hbm,
    wup_hbm,
    wdn_hbm,
    wta_hbm,
    w_pos_out_ref,
    den_ref,
    t_all,
    v_state,
    v_post,
    v_onehot,
    v_tok,
    v_pair,
    v_bias,
    bias_send,
    v_wat,
    v_wqg,
    v_wkv,
    v_wo,
    v_wup,
    v_wdn,
    v_wta,
    v_ids,
    ids_all,
    state_own,
    state_mate,
    sum_send,
    sum_recv,
    rows_own,
    rows_kv,
    q_own,
    q_all,
    v_km,
    v_vm,
    v_p,
    o_send,
    o_recv,
    st_send,
    st_recv,
    v_inner,
    t_own,
    ta_own,
    ta_all,
    load_sem,
    pair_sem,
    ids_sems,
    state_sems,
    sum_sems,
    bias_sems,
    kv_send,
    kv_recv,
    kv_local,
    kvm_sems,
    q_sems,
    o_sems,
    st_sems,
    t_sems,
    tm_sems,
    ta_sems,
):
    atoms = noisy_ref.shape[1]
    atoms_pad = v_state.shape[0]
    tok_rows, cols, channels = v_pair.shape
    heads = bias_w_ref.shape[0]
    half = heads // 2
    own, width = v_tok.shape
    head_dim = width // heads
    span = width // 2
    hidden = v_wdn.shape[0]
    chips = n_ba // 2
    keys_n = 2 * cols
    me_a = lax.axis_index("aa")
    me_b = lax.axis_index("ba")
    core = lax.rem(me_b, 2)
    chip = me_b // 2

    def at(a, b):
        return {"aa": a, "ba": b}

    def greet(device):
        pl.semaphore_signal(barrier, inc=1, device_id=device, device_id_type=MESH)

    barrier = pltpu.get_barrier_semaphore()
    for x in range(1, n_ba):
        greet(at(me_a, flip(me_b, x)))
    for x in range(1, n_aa):
        greet(at(flip(me_a, x), 2 * me_a + core))
    for x in range(1, chips):
        greet(at(chip, flip(me_b, 2 * x)))

    @pl.when(chip != me_a)
    def _():
        greet(at(me_a, 2 * me_a + core))
        greet(at(chip, me_b))

    greetings = n_ba - 1 + n_aa - 1 + chips - 1 + jnp.where(chip != me_a, 2, 0)

    if atoms_pad > atoms:
        v_state[pl.ds(atoms, atoms_pad - atoms), :] = jnp.zeros(
            (atoms_pad - atoms, channels), F32
        )
    own_start = pl.multiple_of(me_b * own, own)
    span_start = pl.multiple_of(core * span, LANES)
    loads = {}
    for slot, (name, src, dst) in enumerate(
        [
            ("ids", ids_hbm, v_ids.at[0]),
            ("atom", atom_hbm, v_state.at[pl.ds(0, atoms)]),
            ("wat", wat_hbm, v_wat),
            ("tok", tok_hbm.at[pl.ds(own_start, own)], v_tok),
            ("wqg", wqg_hbm, v_wqg),
            ("wk", wkv_hbm.at[:, pl.ds(span_start, span)], v_wkv.at[:, pl.ds(0, span)]),
            (
                "wv",
                wkv_hbm.at[:, pl.ds(pl.multiple_of(width + core * span, LANES), span)],
                v_wkv.at[:, pl.ds(span, span)],
            ),
            ("wo", wo_hbm, v_wo),
            ("wup", wup_hbm, v_wup),
            ("wdn", wdn_hbm, v_wdn),
            ("wta", wta_hbm, v_wta),
        ]
    ):
        loads[name] = pltpu.make_async_copy(src, dst, load_sem.at[slot])
    step = tok_rows // PAIR_CHUNKS
    pair_loads = [
        pltpu.make_async_copy(
            pair_hbm.at[pl.ds(c * step, step)], v_pair.at[pl.ds(c * step, step)], pair_sem.at[c]
        )
        for c in range(PAIR_CHUNKS)
    ]
    for name in ("ids", "atom", "wat", "tok"):
        loads[name].start()
    for copy in pair_loads:
        copy.start()
    for name in ("wqg", "wk", "wv", "wo", "wup", "wdn", "wta"):
        loads[name].start()

    def ba_copy(src, dst, sems, x, slot):
        return pltpu.make_async_remote_copy(
            src_ref=src,
            dst_ref=dst,
            send_sem=sems.at[0, slot],
            recv_sem=sems.at[1, slot],
            device_id=at(me_a, flip(me_b, x)),
            device_id_type=MESH,
        )

    order = far_first(n_ba)
    chip_order = far_first(chips)
    sent = []

    def send(copy):
        copy.start()
        sent.append(copy)

    sigma = jnp.full((3, atoms), noise_ref[0], F32)
    inv_scale = 1.0 / jnp.sqrt(sigma * sigma + 1.0)
    v_post[...] = jnp.full(v_post.shape, -1.0, F32)
    v_post[0:3, 0:atoms] = noisy_ref[...] * inv_scale
    loads["ids"].wait()
    ids_row = v_ids[...]
    v_post[3:4, :] = ids_row.astype(F32)
    columns = v_post[...].T
    loads["atom"].wait()
    state = v_state[...]
    for c in range(3):
        state = state + columns[:, c : c + 1] * w_pos_ref[c : c + 1, :]
    v_state[...] = state
    rounded = state.astype(BF16)
    state_own[...] = rounded

    pl.semaphore_wait(barrier, greetings)
    state_copy = ba_copy(state_own, state_mate, state_sems, 1, 0)
    send(state_copy)
    ids_copies = {x: ba_copy(v_ids, ids_all.at[x - 1], ids_sems, x, x - 1) for x in order}
    for x in [1] + [x for x in order if x != 1]:
        send(ids_copies[x])

    def select(ids):
        row = lax.broadcasted_iota(jnp.int32, (chips * own, atoms_pad), 0)
        token = row + own * (row // own) + (own * core + me_a * tok_rows)
        return jnp.where(token == ids, 1.0, 0.0).astype(BF16)

    loads["wat"].wait()
    hidden_atom = jnp.maximum(dot(rounded, v_wat[...]), 0.0).astype(BF16)
    chip_sums = dot(select(ids_row), hidden_atom)
    ids_copies[1].wait_recv()
    selector = select(ids_all[0])
    state_copy.wait_recv()
    hidden_atom = jnp.maximum(dot(state_mate[...], v_wat[...]), 0.0).astype(BF16)
    chip_sums = chip_sums + dot(selector, hidden_atom)
    sum_send[...] = chip_sums.astype(BF16).reshape(chips, own, width)
    sum_copies = {
        d: ba_copy(sum_send.at[flip(chip, d)], sum_recv.at[d - 1], sum_sems, 2 * d, d - 1)
        for d in chip_order
    }
    for d in chip_order:
        send(sum_copies[d])

    lane_id = lax.broadcasted_iota(jnp.int32, (atoms_pad, tok_rows), 1) + me_a * tok_rows
    v_onehot[...] = jnp.where(columns[:, 3:4] == lane_id.astype(F32), 1.0, 0.0).astype(BF16)
    weights_all = bias_w_ref[...].astype(F32)
    first_half, second_half = weights_all[0:half], weights_all[half:heads]
    bias_w = jnp.concatenate(
        [
            jnp.where(core == 0, first_half, second_half),
            jnp.where(core == 0, second_half, first_half),
        ],
        axis=0,
    ).astype(BF16)
    bias_rows = step * half
    bias_copies = [
        ba_copy(
            bias_send.at[pl.ds(c * bias_rows, bias_rows)],
            v_bias.at[core, pl.ds(c * bias_rows, bias_rows)],
            bias_sems,
            1,
            c,
        )
        for c in range(PAIR_CHUNKS)
    ]

    def bias_chunk(c):
        pair_loads[c].wait()

        def rows(r, carry):
            start = c * step + r * BIAS_ROWS
            block = v_pair[pl.ds(start, BIAS_ROWS)].reshape(BIAS_ROWS * cols, channels)
            out = dot_nt(bias_w, block)
            for i in range(BIAS_ROWS):
                where = pl.ds(pl.multiple_of((start + i) * half, half), half)
                v_bias[core, where, :] = out[0:half, i * cols : (i + 1) * cols]
                bias_send[where, :] = out[half:heads, i * cols : (i + 1) * cols]
            return carry

        lax.fori_loop(0, step // BIAS_ROWS, rows, 0)
        send(bias_copies[c])

    for c in range(EARLY_CHUNKS):
        bias_chunk(c)

    own_row = lax.broadcasted_iota(jnp.int32, (own, atoms_pad), 0) + (
        me_a * tok_rows + me_b * own
    )
    hits = jnp.where(own_row == ids_row, 1.0, 0.0)
    for x in order:
        if x != 1:
            ids_copies[x].wait_recv()
        hits = hits + jnp.where(own_row == ids_all[x - 1], 1.0, 0.0)
    counts = jnp.sum(hits, axis=1, keepdims=True)
    summed = sum_send[chip].astype(F32)
    for d in chip_order:
        sum_copies[d].wait_recv()
        summed = summed + sum_recv[d - 1].astype(F32)
    loads["tok"].wait()
    tokens_start = v_tok[...] + summed / counts
    v_tok[...] = tokens_start
    normed = norm(tokens_start, gains_ref[0:1, :]).astype(BF16)
    rows_own[...] = normed

    def kv_copy(x):
        return pltpu.make_async_remote_copy(
            src_ref=rows_own,
            dst_ref=rows_kv.at[me_b],
            send_sem=kv_send.at[x],
            recv_sem=kv_recv.at[chip],
            device_id=at(flip(me_a, x), 2 * me_a + core),
            device_id_type=MESH,
        )

    own_piece = pltpu.make_async_copy(rows_own, rows_kv.at[me_b], kv_local)
    for x in far_first(n_aa):
        send(kv_copy(x))

    @pl.when(chip == me_a)
    def _():
        own_piece.start()

    @pl.when(chip != me_a)
    def _():
        kv_copy(0).start()

    loads["wqg"].wait()
    query = dot(normed, v_wqg[:, 0:width]).astype(BF16)
    for c in range(2):
        q_own[c] = query[:, c * span : (c + 1) * span]
    q_all[me_b] = q_own[core]
    q_copies = {
        x: ba_copy(q_own.at[lax.rem(core + x, 2)], q_all.at[me_b], q_sems, x, x - 1)
        for x in order
    }
    for x in order:
        send(q_copies[x])
    gate = jax.nn.sigmoid(dot(normed, v_wqg[:, width : 2 * width])).astype(BF16)

    for c in range(EARLY_CHUNKS, PAIR_CHUNKS):
        bias_chunk(c)
    mate_rows = {}
    for d in range(chips):
        piece = flip(me_b, 2 * d)
        source = pltpu.make_async_remote_copy(
            src_ref=rows_own,
            dst_ref=rows_kv.at[piece],
            send_sem=kv_send.at[0],
            recv_sem=kv_recv.at[flip(chip, d)],
            device_id=at(chip, piece),
            device_id_type=MESH,
        )
        if d == 0:

            @pl.when(chip == me_a)
            def _():
                own_piece.wait()

            @pl.when(chip != me_a)
            def _():
                source.wait_recv()
        else:
            source.wait_recv()
        mate_rows[d] = ba_copy(rows_kv.at[piece], rows_kv.at[piece], kvm_sems, 1, d)
        send(mate_rows[d])
    loads["wk"].wait()
    loads["wv"].wait()
    for d in range(chips):
        mate_rows[d].wait_recv()

    key_value = dot(rows_kv[...].reshape(keys_n, width), v_wkv[...])
    spans = []
    for h in range(half):
        lo = h * head_dim // LANES * LANES
        hi = ((h + 1) * head_dim + LANES - 1) // LANES * LANES
        spans.append((lo, hi))
        lane = lax.broadcasted_iota(jnp.int32, (keys_n, hi - lo), 1) + lo
        mine = (lane >= h * head_dim) & (lane < (h + 1) * head_dim)
        v_km[h, :, 0 : hi - lo] = jnp.where(mine, key_value[:, lo:hi], 0.0).astype(BF16)
    tiles = []
    for t in range(span // LANES):
        h0 = t * LANES // head_dim
        h1 = (t * LANES + LANES - 1) // head_dim
        tiles.append((h0, h1))
        part = key_value[:, span + t * LANES : span + (t + 1) * LANES]
        lane = lax.broadcasted_iota(jnp.int32, (keys_n, LANES), 1) + t * LANES
        for h in range(h0, h1 + 1):
            mine = (lane >= h * head_dim) & (lane < (h + 1) * head_dim)
            v_vm[t, (h - h0) * keys_n : (h - h0 + 1) * keys_n, :] = jnp.where(
                mine, part, 0.0
            ).astype(BF16)

    for x in order:
        q_copies[x].wait_recv()
    for c in range(PAIR_CHUNKS):
        bias_copies[c].wait_recv()

    scale = head_dim ** (-0.5)
    rows2 = 2 * own
    lane = lax.broadcasted_iota(jnp.int32, (rows2, LANES), 1)
    top_lane = lane - half * core
    groups = own // 8
    o_copies = {
        x: ba_copy(o_send.at[flip(me_b, x)], o_recv.at[x - 1], o_sems, x, x - 1) for x in order
    }
    st_copies = {
        x: ba_copy(st_send.at[flip(me_b, x)], st_recv.at[x - 1], st_sems, x, x - 1)
        for x in order
    }
    for d in chip_order + [0]:
        duo = flip(chip, d)
        stats = jnp.zeros((rows2, LANES), F32)
        q_rows = q_all[pl.ds(2 * duo, 2)].reshape(rows2, span)
        for h in range(half):
            lo, hi = spans[h]
            scores = dot_nt(q_rows[:, lo:hi], v_km[h, :, 0 : hi - lo]) * scale
            where = pl.ds(duo * (rows2 * half) + h, rows2, stride=half)
            parts = [
                scores[:, k * cols : (k + 1) * cols] + v_bias[k, where, :] for k in range(2)
            ]
            top = jnp.max(jnp.maximum(parts[0], parts[1]), axis=1, keepdims=True)
            parts = [jnp.exp(part - top) for part in parts]
            total = jnp.sum(parts[0] + parts[1], axis=1, keepdims=True)
            stats = jnp.where(top_lane == h, top, stats)
            stats = jnp.where(top_lane == heads + h, total, stats)
            for k in range(2):
                v_p[:, h * keys_n + k * cols : h * keys_n + (k + 1) * cols] = parts[k].astype(
                    BF16
                )
        for t, (h0, h1) in enumerate(tiles):
            out = dot(
                v_p[:, h0 * keys_n : (h1 + 1) * keys_n], v_vm[t, 0 : (h1 - h0 + 1) * keys_n, :]
            )
            o_send[pl.ds(2 * duo, 2), :, t * LANES : (t + 1) * LANES] = out.astype(BF16).reshape(
                2, own, LANES
            )
        for c in range(2):
            packed = stats[c * own : c * own + 8]
            for g in range(1, groups):
                piece = pltpu.roll(stats[c * own + 8 * g : c * own + 8 * g + 8], 2 * heads * g, 1)
                packed = jnp.where(lane[0:8] >= 2 * heads * g, piece, packed)
            st_send[2 * duo + c] = packed
        for x in (2 * d + 1, 2 * d):
            if x:
                send(st_copies[x])
                send(o_copies[x])

    def unpack(packed):
        parts = [packed]
        for g in range(1, groups):
            parts.append(pltpu.roll(packed, LANES - 2 * heads * g, 1))
        return jnp.concatenate(parts, axis=0)

    tops = []
    for d in range(chips):
        if d:
            st_copies[2 * d].wait_recv()
        st_copies[2 * d + 1].wait_recv()
        mine = st_recv[2 * d - 1] if d else st_send[me_b]
        tops.append(unpack(mine + st_recv[2 * d]))
    overall = tops[0]
    for top in tops[1:]:
        overall = jnp.maximum(overall, top)
    factors = [jnp.exp(top - overall) for top in tops]
    denominator = jnp.zeros((own, LANES), F32)
    for factor, top in zip(factors, tops):
        denominator = denominator + factor * pltpu.roll(top, LANES - heads, 1)
    head_row = lax.broadcasted_iota(jnp.int32, (LANES, width), 0)
    head_lane = lax.broadcasted_iota(jnp.int32, (LANES, width), 1)
    inside = (head_lane >= head_row * head_dim) & (head_lane < (head_row + 1) * head_dim)
    spread = jnp.where(inside, 1.0, 0.0).astype(BF16)
    live = lane[0:own] < heads
    shares = jnp.concatenate(
        [jnp.where(live, factor / denominator, 0.0) for factor in factors], axis=0
    )
    coarse = shares.astype(BF16)
    fine = (shares - coarse.astype(F32)).astype(BF16)
    wide = dot(coarse, spread) + dot(fine, spread)
    left = jnp.zeros((own, span), F32)
    right = jnp.zeros((own, span), F32)
    for d in range(chips):
        if d:
            o_copies[2 * d].wait_recv()
        o_copies[2 * d + 1].wait_recv()
        mine = (o_recv[2 * d - 1] if d else o_send[me_b]).astype(F32)
        other = o_recv[2 * d].astype(F32)
        part = wide[d * own : (d + 1) * own]
        left = left + part[:, 0:span] * jnp.where(core == 0, mine, other)
        right = right + part[:, span:width] * jnp.where(core == 0, other, mine)
    attended = jnp.concatenate([left, right], axis=1)
    mixed = (attended * gate.astype(F32)).astype(BF16)
    loads["wo"].wait()
    tokens_mid = v_tok[...] + dot(mixed, v_wo[...])
    normed_mid = norm(tokens_mid, gains_ref[1:2, :]).astype(BF16)
    loads["wup"].wait()
    part = 512
    for n in range(0, hidden, part):
        first = dot(normed_mid, v_wup[:, n : n + part])
        second = dot(normed_mid, v_wup[:, hidden + n : hidden + n + part])
        v_inner[:, n : n + part] = (first * jax.nn.sigmoid(first) * second).astype(BF16)
    loads["wdn"].wait()
    token_out = tokens_mid + dot(v_inner[...], v_wdn[...])
    token_round = token_out.astype(BF16)
    t_own[...] = token_round
    t_all[me_b] = token_round
    loads["wta"].wait()
    normed_out = norm(token_out, gains_ref[2:3, :]).astype(BF16)
    token_atom = dot(normed_out, v_wta[...]).astype(BF16)
    ta_own[...] = token_atom
    ta_all[me_b] = token_atom
    ta_copies = {x: ba_copy(ta_own, ta_all.at[me_b], ta_sems, x, x - 1) for x in order}
    for x in order:
        send(ta_copies[x])
    t_copies = {
        d: ba_copy(t_own, t_all.at[me_b], t_sems, 2 * d, d - 1) for d in chip_order
    }
    for d in chip_order:
        send(t_copies[d])
    tm_copies = {0: ba_copy(t_own, t_all.at[me_b], tm_sems, 1, 0)}
    send(tm_copies[0])
    for x in order:
        ta_copies[x].wait_recv()
    picked = dot(v_onehot[...], ta_all[...].reshape(tok_rows, channels))
    atom_normed = norm(v_state[...] + picked, None).astype(BF16)
    update = dot_nt(w_pos_out_ref[...], atom_normed)[:, 0:atoms]
    den_ref[...] = noisy_ref[...] * (inv_scale * inv_scale) + update * (sigma * inv_scale)
    for d in range(1, chips):
        piece = flip(me_b, 2 * d)
        t_copies[d].wait_recv()
        tm_copies[d] = ba_copy(t_all.at[piece], t_all.at[piece], tm_sems, 1, d)
        send(tm_copies[d])
    for d in range(chips):
        tm_copies[d].wait_recv()
    for copy in sent:
        copy.wait_send()

    @pl.when(chip != me_a)
    def _():
        kv_copy(0).wait_send()


def finish_kernel(tok_ref, den_ref, den_out_ref, tok_out_ref):
    den_out_ref[...] = den_ref[...]
    tok_out_ref[...] = tok_ref[...].astype(F32)


def on_device(
    n_aa,
    n_ba,
    atom_cond,
    noisy_pos,
    noise_level,
    atom_token,
    token_cond,
    pair,
    pair_bias_weight,
    gains,
    w_pos,
    w_atom_token,
    w_query_gate,
    w_key_value,
    w_attn_out,
    w_up,
    w_down,
    w_token_atom,
    w_pos_out,
):
    atoms, channels = atom_cond.shape
    atoms_pad = -(-atoms // LANES) * LANES
    tok_rows, width = token_cond.shape
    cols = pair.shape[1]
    heads = pair_bias_weight.shape[0]
    own = tok_rows // n_ba
    chips = n_ba // 2
    half, span, keys_n = heads // 2, width // 2, 2 * cols
    head_dim = width // heads
    if tok_rows != 2 * cols or chips != n_aa:
        raise ValueError("unsupported mesh")
    tile_heads = max(
        (t * LANES + LANES - 1) // head_dim - t * LANES // head_dim + 1
        for t in range(span // LANES)
    )
    ids = atom_token
    if atoms_pad > atoms:
        ids = jnp.pad(atom_token, (0, atoms_pad - atoms), constant_values=-1)
    vmem = pl.BlockSpec(memory_space=pltpu.VMEM)
    smem = pl.BlockSpec(memory_space=pltpu.SMEM)
    hbm = pl.BlockSpec(memory_space=pltpu.HBM)
    dma = pltpu.SemaphoreType.DMA
    operands = [
        pltpu.with_memory_space_constraint(value, pltpu.HBM) if value.size > 1 else value
        for value in (
            atom_cond,
            noisy_pos,
            noise_level,
            ids,
            token_cond,
            pair,
            pair_bias_weight,
            gains,
            w_pos,
            w_atom_token,
            w_query_gate,
            w_key_value,
            w_attn_out,
            w_up,
            w_down,
            w_token_atom,
            w_pos_out,
        )
    ]
    denoised, tokens = pl.pallas_call(
        functools.partial(step_kernel, n_aa, n_ba),
        out_shape=[
            jax.ShapeDtypeStruct((3, atoms), F32),
            jax.ShapeDtypeStruct((n_ba, own, width), BF16),
        ],
        in_specs=[hbm, vmem, smem, hbm, hbm, hbm, vmem, vmem, vmem] + [hbm] * 7 + [vmem],
        out_specs=[vmem, vmem],
        scratch_shapes=[
            pltpu.VMEM((atoms_pad, channels), F32),
            pltpu.VMEM((LANES, atoms_pad), F32),
            pltpu.VMEM((atoms_pad, tok_rows), BF16),
            pltpu.VMEM((own, width), F32),
            pltpu.VMEM(pair.shape, BF16),
            pltpu.VMEM((2, tok_rows * half, cols), F32),
            pltpu.VMEM((tok_rows * half, cols), F32),
            pltpu.VMEM(w_atom_token.shape, BF16),
            pltpu.VMEM(w_query_gate.shape, BF16),
            pltpu.VMEM((width, width), BF16),
            pltpu.VMEM(w_attn_out.shape, BF16),
            pltpu.VMEM(w_up.shape, BF16),
            pltpu.VMEM(w_down.shape, BF16),
            pltpu.VMEM(w_token_atom.shape, BF16),
            pltpu.VMEM((1, atoms_pad), jnp.int32),
            pltpu.VMEM((n_ba - 1, 1, atoms_pad), jnp.int32),
            pltpu.VMEM((atoms_pad, channels), BF16),
            pltpu.VMEM((atoms_pad, channels), BF16),
            pltpu.VMEM((chips, own, width), BF16),
            pltpu.VMEM((chips - 1, own, width), BF16),
            pltpu.VMEM((own, width), BF16),
            pltpu.VMEM((n_ba, own, width), BF16),
            pltpu.VMEM((2, own, span), BF16),
            pltpu.VMEM((n_ba, own, span), BF16),
            pltpu.VMEM((half, keys_n, 2 * LANES), BF16),
            pltpu.VMEM((span // LANES, tile_heads * keys_n, LANES), BF16),
            pltpu.VMEM((2 * own, half * keys_n), BF16),
            pltpu.VMEM((n_ba, own, span), BF16),
            pltpu.VMEM((n_ba - 1, own, span), BF16),
            pltpu.VMEM((n_ba, 8, LANES), F32),
            pltpu.VMEM((n_ba - 1, 8, LANES), F32),
            pltpu.VMEM((own, w_down.shape[0]), BF16),
            pltpu.VMEM((own, width), BF16),
            pltpu.VMEM((own, channels), BF16),
            pltpu.VMEM((n_ba, own, channels), BF16),
            dma((11,)),
            dma((PAIR_CHUNKS,)),
            dma((2, n_ba - 1)),
            dma((2, 1)),
            dma((2, chips - 1)),
            dma((2, PAIR_CHUNKS)),
            dma((n_aa,)),
            dma((chips,)),
            dma,
            dma((2, chips)),
            dma((2, n_ba - 1)),
            dma((2, n_ba - 1)),
            dma((2, n_ba - 1)),
            dma((2, chips - 1)),
            dma((2, chips)),
            dma((2, n_ba - 1)),
        ],
        compiler_params=pltpu.CompilerParams(
            collective_id=0, has_side_effects=True, vmem_limit_bytes=48 * 1024 * 1024
        ),
    )(*operands)
    denoised, token_out = pl.pallas_call(
        finish_kernel,
        out_shape=[
            jax.ShapeDtypeStruct((3, atoms), F32),
            jax.ShapeDtypeStruct((tok_rows, width), F32),
        ],
        in_specs=[vmem, vmem],
        out_specs=[vmem, vmem],
        compiler_params=pltpu.CompilerParams(vmem_limit_bytes=8 * 1024 * 1024),
    )(tokens.reshape(tok_rows, width), denoised)
    return denoised, token_out


def solution(mesh):
    in_specs = (
        P(("aa", "ba"), None),
        P(None, ("aa", "ba")),
        P(),
        P(("aa", "ba")),
        P("aa", None),
        P("aa", "ba", None),
    ) + (P(),) * 11
    out_specs = (P(None, ("aa", "ba")), P("aa", None))
    return jax.shard_map(
        functools.partial(on_device, mesh.shape["aa"], mesh.shape["ba"]),
        mesh=mesh,
        in_specs=in_specs,
        out_specs=out_specs,
        check_vma=False,
    )
```

time: 47.7 us -> 38 us (0.80)
  Pallas kernels: 41.7 us -> 36.5 us
  local copies, waits for them, and re-layouts: 2.53 us -> 0 us
  other arithmetic: 1.93 us -> 0 us
    pallas_call x1, Pallas kernels: 41.7 us -> 35.5 us  [on_device(): pl.pallas_call(functools.partial(step_kernel, n_aa, n_ba), out_shape=[jax...]
    convert_element_type x1 -> x0, other arithmetic: 1.93 us -> none  [on_device(): return (denoised, tokens.reshape(tok_rows, width).astype(F32))]
    unnamed x1 -> x0, local copies, waits for them, and re-layouts: 1.29 us -> none
    reshape x1 -> x0, local copies, waits for them, and re-layouts: 1.25 us -> none  [on_device(): atom_token.reshape(1, -1)]
    pallas_call x0 -> x1, Pallas kernels: none -> 0.93 us  [on_device(): pl.pallas_call(finish_kernel, out_shape=[jax.ShapeDtypeStruct((3, atoms),...]
where the time goes in v2:
time: 38 us; the launch traced here: 37.8 us
  Pallas kernels  36.5 us (96%)
  between operations  1.29 us (3%)
    pallas_call x1, Pallas kernels, on_device(): pl.pallas_call(functools.partial(step_kernel, n_aa, n_ba), out_shape=[jax...  35.5 us
    pallas_call x1, Pallas kernels, on_device(): pl.pallas_call(finish_kernel, out_shape=[jax.ShapeDtypeStruct((3, atoms),...  0.93 us

profile of v2, /device:TPU:0, one launch (start us, length us, event | category | flops | bytes accessed | tf_op | source)
XLA Modules:
  0.0 37.8 jit_solution(8507386487163258663)
XLA Ops:
  1.3 35.5 %shard_map.176 = (f32[3,384]{1,0:T(4,128)S(1)}, bf16[8,32,768]{2,1,0:T(8,128)(2,1)S(1)}) custom-call(f32[384,128]{1,0:T(8,128)} %atom_hbm.1, f32[3,384]{1,0:T(4,128)} %noisy_ref.1, f32[1]{0:T(128)S(6)} %copy.19.noise_ref, s32[384]{0:T(512)} %ids_hbm.1, f32[256,768]{1,0:T(8,128)} %tok_hbm.1, bf16[256,128,128]{2,1,0:T(8,128)(2,1)} %pair_hbm.1, ...), custom_call_target="tpu_custom_call" | custom-call | tf_op jit(solution)/shard_map/pallas_call | solution.py:631
  36.8 0.9 %shard_map.177 = (f32[3,384]{1,0:T(4,128)}, f32[256,768]{1,0:T(8,128)}) custom-call(bf16[256,768]{1,0:T(8,128)(2,1)S(1)} %bitcast.1, f32[3,384]{1,0:T(4,128)S(1)} %get-tuple-element.5.den_ref), custom_call_target="tpu_custom_call" | custom-call | tf_op jit(solution)/shard_map/pallas_call | solution.py:696

commit v3 on v2

--- a/solution.py
+++ b/solution.py
@@ -11,8 +11,8 @@
 F32 = jnp.float32
 BF16 = jnp.bfloat16
 LANES = 128
-PAIR_CHUNKS = 8
-EARLY_CHUNKS = 4
+PAIR_CHUNKS = 4
+EARLY_CHUNKS = 2
 BIAS_ROWS = 8
 
 
@@ -50,14 +50,14 @@
     n_aa,
     n_ba,
     atom_hbm,
-    noisy_ref,
+    noisy_hbm,
     noise_ref,
     ids_hbm,
     tok_hbm,
     pair_hbm,
-    bias_w_ref,
-    gains_ref,
-    w_pos_ref,
+    bias_w_hbm,
+    gains_hbm,
+    w_pos_hbm,
     wat_hbm,
     wqg_hbm,
     wkv_hbm,
@@ -65,9 +65,14 @@
     wup_hbm,
     wdn_hbm,
     wta_hbm,
-    w_pos_out_ref,
+    w_pos_out_hbm,
     den_ref,
     t_all,
+    noisy_ref,
+    bias_w_ref,
+    gains_ref,
+    w_pos_ref,
+    w_pos_out_ref,
     v_state,
     v_post,
     v_onehot,
@@ -78,11 +83,11 @@
     v_wat,
     v_wqg,
     v_wkv,
-    v_wo,
+    v_wod,
     v_wup,
-    v_wdn,
     v_wta,
     v_ids,
+    ids_mate,
     ids_all,
     state_own,
     state_mate,
@@ -105,6 +110,7 @@
     ta_all,
     load_sem,
     pair_sem,
+    ids_mate_sems,
     ids_sems,
     state_sems,
     sum_sems,
@@ -128,13 +134,61 @@
     own, width = v_tok.shape
     head_dim = width // heads
     span = width // 2
-    hidden = v_wdn.shape[0]
+    hidden = v_wod.shape[0] - width
+    halves, half_rows = rows_own.shape[:2]
     chips = n_ba // 2
     keys_n = 2 * cols
     me_a = lax.axis_index("aa")
     me_b = lax.axis_index("ba")
     core = lax.rem(me_b, 2)
     chip = me_b // 2
+
+    own_start = pl.multiple_of(me_b * own, own)
+    span_start = pl.multiple_of(core * span, LANES)
+    copies = [
+        ("ids", ids_hbm, v_ids.at[0]),
+        ("noisy", noisy_hbm, noisy_ref),
+        ("atom", atom_hbm, v_state.at[pl.ds(0, atoms)]),
+        ("w_pos", w_pos_hbm, w_pos_ref),
+        ("wat", wat_hbm, v_wat),
+        ("bias_w", bias_w_hbm, bias_w_ref),
+        ("gains", gains_hbm, gains_ref),
+        ("tok", tok_hbm.at[pl.ds(own_start, own)], v_tok),
+        ("w_pos_out", w_pos_out_hbm, w_pos_out_ref),
+        ("wqg", wqg_hbm, v_wqg),
+        ("wkv", wkv_hbm.at[:, pl.ds(span_start, span)], v_wkv.at[:, pl.ds(0, span)]),
+        (
+            "wkv",
+            wkv_hbm.at[:, pl.ds(pl.multiple_of(width + core * span, LANES), span)],
+            v_wkv.at[:, pl.ds(span, span)],
+        ),
+        ("wod", wo_hbm, v_wod.at[pl.ds(0, width)]),
+        ("wup", wup_hbm, v_wup),
+        ("wod", wdn_hbm, v_wod.at[pl.ds(width, hidden)]),
+        ("wta", wta_hbm, v_wta),
+    ]
+    names = list(dict.fromkeys(name for name, _, _ in copies))
+
+    def load(name):
+        for key, src, dst in copies:
+            if key == name:
+                pltpu.make_async_copy(src, dst, load_sem.at[names.index(name)]).start()
+
+    def take(whole, sem):
+        pltpu.make_async_copy(whole, whole, sem).wait()
+
+    def loaded(name, whole):
+        take(whole, load_sem.at[names.index(name)])
+
+    step = tok_rows // PAIR_CHUNKS
+    pair_loads = [
+        pltpu.make_async_copy(
+            pair_hbm.at[pl.ds(c * step, step)], v_pair.at[pl.ds(c * step, step)], pair_sem.at[c]
+        )
+        for c in range(PAIR_CHUNKS)
+    ]
+    for name in names[:5]:
+        load(name)
 
     def at(a, b):
         return {"aa": a, "ba": b}
@@ -157,74 +211,41 @@
 
     greetings = n_ba - 1 + n_aa - 1 + chips - 1 + jnp.where(chip != me_a, 2, 0)
 
+    for name in names[5:8]:
+        load(name)
+    for copy in pair_loads:
+        copy.start()
+    for name in names[8:]:
+        load(name)
     if atoms_pad > atoms:
         v_state[pl.ds(atoms, atoms_pad - atoms), :] = jnp.zeros(
             (atoms_pad - atoms, channels), F32
         )
-    own_start = pl.multiple_of(me_b * own, own)
-    span_start = pl.multiple_of(core * span, LANES)
-    loads = {}
-    for slot, (name, src, dst) in enumerate(
-        [
-            ("ids", ids_hbm, v_ids.at[0]),
-            ("atom", atom_hbm, v_state.at[pl.ds(0, atoms)]),
-            ("wat", wat_hbm, v_wat),
-            ("tok", tok_hbm.at[pl.ds(own_start, own)], v_tok),
-            ("wqg", wqg_hbm, v_wqg),
-            ("wk", wkv_hbm.at[:, pl.ds(span_start, span)], v_wkv.at[:, pl.ds(0, span)]),
-            (
-                "wv",
-                wkv_hbm.at[:, pl.ds(pl.multiple_of(width + core * span, LANES), span)],
-                v_wkv.at[:, pl.ds(span, span)],
-            ),
-            ("wo", wo_hbm, v_wo),
-            ("wup", wup_hbm, v_wup),
-            ("wdn", wdn_hbm, v_wdn),
-            ("wta", wta_hbm, v_wta),
-        ]
-    ):
-        loads[name] = pltpu.make_async_copy(src, dst, load_sem.at[slot])
-    step = tok_rows // PAIR_CHUNKS
-    pair_loads = [
-        pltpu.make_async_copy(
-            pair_hbm.at[pl.ds(c * step, step)], v_pair.at[pl.ds(c * step, step)], pair_sem.at[c]
-        )
-        for c in range(PAIR_CHUNKS)
-    ]
-    for name in ("ids", "atom", "wat", "tok"):
-        loads[name].start()
-    for copy in pair_loads:
-        copy.start()
-    for name in ("wqg", "wk", "wv", "wo", "wup", "wdn", "wta"):
-        loads[name].start()
-
-    def ba_copy(src, dst, sems, x, slot):
+
+    def ba_copy(src, dst, sems, x, slot=1):
         return pltpu.make_async_remote_copy(
             src_ref=src,
             dst_ref=dst,
-            send_sem=sems.at[0, slot],
-            recv_sem=sems.at[1, slot],
+            send_sem=sems.at[0],
+            recv_sem=sems.at[slot],
             device_id=at(me_a, flip(me_b, x)),
             device_id_type=MESH,
         )
 
     order = far_first(n_ba)
     chip_order = far_first(chips)
-    sent = []
-
-    def send(copy):
-        copy.start()
-        sent.append(copy)
-
+
+    loaded("noisy", noisy_ref)
     sigma = jnp.full((3, atoms), noise_ref[0], F32)
     inv_scale = 1.0 / jnp.sqrt(sigma * sigma + 1.0)
     v_post[...] = jnp.full(v_post.shape, -1.0, F32)
     v_post[0:3, 0:atoms] = noisy_ref[...] * inv_scale
-    loads["ids"].wait()
+    loaded("ids", v_ids.at[0])
     ids_row = v_ids[...]
     v_post[3:4, :] = ids_row.astype(F32)
     columns = v_post[...].T
-    loads["atom"].wait()
+    loaded("w_pos", w_pos_ref)
+    loaded("atom", v_state.at[pl.ds(0, atoms)])
     state = v_state[...]
     for c in range(3):
         state = state + columns[:, c : c + 1] * w_pos_ref[c : c + 1, :]
@@ -233,35 +254,39 @@
     state_own[...] = rounded
 
     pl.semaphore_wait(barrier, greetings)
-    state_copy = ba_copy(state_own, state_mate, state_sems, 1, 0)
-    send(state_copy)
-    ids_copies = {x: ba_copy(v_ids, ids_all.at[x - 1], ids_sems, x, x - 1) for x in order}
-    for x in [1] + [x for x in order if x != 1]:
-        send(ids_copies[x])
-
-    def select(ids):
-        row = lax.broadcasted_iota(jnp.int32, (chips * own, atoms_pad), 0)
-        token = row + own * (row // own) + (own * core + me_a * tok_rows)
+    ba_copy(state_own, state_mate, state_sems, 1).start()
+    ba_copy(v_ids, ids_mate, ids_mate_sems, 1).start()
+    for x in order:
+        ba_copy(v_ids, ids_all.at[x - 1], ids_sems, x).start()
+
+    def select(ids, part):
+        row = lax.broadcasted_iota(jnp.int32, (chips * half_rows, atoms_pad), 0)
+        token = lax.rem(row, half_rows) + 2 * own * (row // half_rows)
+        token = token + (own * core + me_a * tok_rows + part * half_rows)
         return jnp.where(token == ids, 1.0, 0.0).astype(BF16)
 
-    loads["wat"].wait()
-    hidden_atom = jnp.maximum(dot(rounded, v_wat[...]), 0.0).astype(BF16)
-    chip_sums = dot(select(ids_row), hidden_atom)
-    ids_copies[1].wait_recv()
-    selector = select(ids_all[0])
-    state_copy.wait_recv()
-    hidden_atom = jnp.maximum(dot(state_mate[...], v_wat[...]), 0.0).astype(BF16)
-    chip_sums = chip_sums + dot(selector, hidden_atom)
-    sum_send[...] = chip_sums.astype(BF16).reshape(chips, own, width)
-    sum_copies = {
-        d: ba_copy(sum_send.at[flip(chip, d)], sum_recv.at[d - 1], sum_sems, 2 * d, d - 1)
-        for d in chip_order
-    }
-    for d in chip_order:
-        send(sum_copies[d])
+    loaded("wat", v_wat)
+    hidden_own = jnp.maximum(dot(rounded, v_wat[...]), 0.0).astype(BF16)
+    own_sums = [dot(select(ids_row, part), hidden_own) for part in range(halves)]
+    take(ids_mate, ids_mate_sems.at[1])
+    selectors = [select(ids_mate[...], part) for part in range(halves)]
+    take(state_mate, state_sems.at[1])
+    hidden_mate = jnp.maximum(dot(state_mate[...], v_wat[...]), 0.0).astype(BF16)
+    for part in range(halves):
+        chip_sums = own_sums[part] + dot(selectors[part], hidden_mate)
+        sum_send[part] = chip_sums.astype(BF16).reshape(chips, half_rows, width)
+        for d in chip_order:
+            ba_copy(
+                sum_send.at[part, flip(chip, d)],
+                sum_recv.at[part, d - 1],
+                sum_sems,
+                2 * d,
+                1 + part,
+            ).start()
 
     lane_id = lax.broadcasted_iota(jnp.int32, (atoms_pad, tok_rows), 1) + me_a * tok_rows
     v_onehot[...] = jnp.where(columns[:, 3:4] == lane_id.astype(F32), 1.0, 0.0).astype(BF16)
+    loaded("bias_w", bias_w_ref)
     weights_all = bias_w_ref[...].astype(F32)
     first_half, second_half = weights_all[0:half], weights_all[half:heads]
     bias_w = jnp.concatenate(
@@ -278,7 +303,6 @@
             v_bias.at[core, pl.ds(c * bias_rows, bias_rows)],
             bias_sems,
             1,
-            c,
         )
         for c in range(PAIR_CHUNKS)
     ]
@@ -297,7 +321,7 @@
             return carry
 
         lax.fori_loop(0, step // BIAS_ROWS, rows, 0)
-        send(bias_copies[c])
+        bias_copies[c].start()
 
     for c in range(EARLY_CHUNKS):
         bias_chunk(c)
@@ -305,87 +329,81 @@
     own_row = lax.broadcasted_iota(jnp.int32, (own, atoms_pad), 0) + (
         me_a * tok_rows + me_b * own
     )
+    take(ids_all, ids_sems.at[1])
     hits = jnp.where(own_row == ids_row, 1.0, 0.0)
     for x in order:
-        if x != 1:
-            ids_copies[x].wait_recv()
         hits = hits + jnp.where(own_row == ids_all[x - 1], 1.0, 0.0)
     counts = jnp.sum(hits, axis=1, keepdims=True)
-    summed = sum_send[chip].astype(F32)
-    for d in chip_order:
-        sum_copies[d].wait_recv()
-        summed = summed + sum_recv[d - 1].astype(F32)
-    loads["tok"].wait()
-    tokens_start = v_tok[...] + summed / counts
-    v_tok[...] = tokens_start
-    normed = norm(tokens_start, gains_ref[0:1, :]).astype(BF16)
-    rows_own[...] = normed
-
-    def kv_copy(x):
+    loaded("tok", v_tok)
+    loaded("gains", gains_ref)
+
+    def kv_copy(x, part):
         return pltpu.make_async_remote_copy(
-            src_ref=rows_own,
-            dst_ref=rows_kv.at[me_b],
-            send_sem=kv_send.at[x],
-            recv_sem=kv_recv.at[chip],
+            src_ref=rows_own.at[part],
+            dst_ref=rows_kv.at[me_b, part],
+            send_sem=kv_send.at[1 if x else 0],
+            recv_sem=kv_recv.at[part, chip],
             device_id=at(flip(me_a, x), 2 * me_a + core),
             device_id_type=MESH,
         )
 
     own_piece = pltpu.make_async_copy(rows_own, rows_kv.at[me_b], kv_local)
-    for x in far_first(n_aa):
-        send(kv_copy(x))
+    for part in range(halves):
+        rows = pl.ds(part * half_rows, half_rows)
+        summed = sum_send[part, chip].astype(F32)
+        take(sum_recv.at[part], sum_sems.at[1 + part])
+        for d in chip_order:
+            summed = summed + sum_recv[part, d - 1].astype(F32)
+        tokens_start = (
+            v_tok[rows, :] + summed / counts[part * half_rows : (part + 1) * half_rows]
+        )
+        v_tok[rows, :] = tokens_start
+        rows_own[part] = norm(tokens_start, gains_ref[0:1, :]).astype(BF16)
+        for x in far_first(n_aa):
+            kv_copy(x, part).start()
+
+        @pl.when(chip != me_a)
+        def _():
+            kv_copy(0, part).start()
 
     @pl.when(chip == me_a)
     def _():
         own_piece.start()
 
-    @pl.when(chip != me_a)
-    def _():
-        kv_copy(0).start()
-
-    loads["wqg"].wait()
+    normed = rows_own[...].reshape(own, width)
+    loaded("wqg", v_wqg)
     query = dot(normed, v_wqg[:, 0:width]).astype(BF16)
     for c in range(2):
         q_own[c] = query[:, c * span : (c + 1) * span]
     q_all[me_b] = q_own[core]
-    q_copies = {
-        x: ba_copy(q_own.at[lax.rem(core + x, 2)], q_all.at[me_b], q_sems, x, x - 1)
-        for x in order
-    }
     for x in order:
-        send(q_copies[x])
+        ba_copy(q_own.at[lax.rem(core + x, 2)], q_all.at[me_b], q_sems, x).start()
     gate = jax.nn.sigmoid(dot(normed, v_wqg[:, width : 2 * width])).astype(BF16)
 
     for c in range(EARLY_CHUNKS, PAIR_CHUNKS):
         bias_chunk(c)
-    mate_rows = {}
-    for d in range(chips):
-        piece = flip(me_b, 2 * d)
-        source = pltpu.make_async_remote_copy(
-            src_ref=rows_own,
-            dst_ref=rows_kv.at[piece],
-            send_sem=kv_send.at[0],
-            recv_sem=kv_recv.at[flip(chip, d)],
-            device_id=at(chip, piece),
-            device_id_type=MESH,
-        )
-        if d == 0:
-
-            @pl.when(chip == me_a)
-            def _():
-                own_piece.wait()
-
-            @pl.when(chip != me_a)
-            def _():
-                source.wait_recv()
-        else:
-            source.wait_recv()
-        mate_rows[d] = ba_copy(rows_kv.at[piece], rows_kv.at[piece], kvm_sems, 1, d)
-        send(mate_rows[d])
-    loads["wk"].wait()
-    loads["wv"].wait()
-    for d in range(chips):
-        mate_rows[d].wait_recv()
+
+    @pl.when(chip == me_a)
+    def _():
+        own_piece.wait()
+
+    for part in range(halves):
+        for d in range(chips):
+            piece = flip(me_b, 2 * d)
+            rows = rows_kv.at[piece, part]
+            arrival = kv_recv.at[part, flip(chip, d)]
+            if d:
+                take(rows, arrival)
+            else:
+
+                @pl.when(chip != me_a)
+                def _():
+                    take(rows, arrival)
+
+            ba_copy(rows, rows, kvm_sems, 1).start()
+    loaded("wkv", v_wkv)
+    chip_pieces = rows_kv.at[pl.ds(0, chips)]
+    take(chip_pieces, kvm_sems.at[1])
 
     key_value = dot(rows_kv[...].reshape(keys_n, width), v_wkv[...])
     spans = []
@@ -409,23 +427,15 @@
                 mine, part, 0.0
             ).astype(BF16)
 
-    for x in order:
-        q_copies[x].wait_recv()
-    for c in range(PAIR_CHUNKS):
-        bias_copies[c].wait_recv()
+    q_pieces = q_all.at[pl.ds(0, n_ba - 1)]
+    take(q_pieces, q_sems.at[1])
+    take(bias_send, bias_sems.at[1])
 
     scale = head_dim ** (-0.5)
     rows2 = 2 * own
     lane = lax.broadcasted_iota(jnp.int32, (rows2, LANES), 1)
     top_lane = lane - half * core
     groups = own // 8
-    o_copies = {
-        x: ba_copy(o_send.at[flip(me_b, x)], o_recv.at[x - 1], o_sems, x, x - 1) for x in order
-    }
-    st_copies = {
-        x: ba_copy(st_send.at[flip(me_b, x)], st_recv.at[x - 1], st_sems, x, x - 1)
-        for x in order
-    }
     for d in chip_order + [0]:
         duo = flip(chip, d)
         stats = jnp.zeros((rows2, LANES), F32)
@@ -461,8 +471,9 @@
             st_send[2 * duo + c] = packed
         for x in (2 * d + 1, 2 * d):
             if x:
-                send(st_copies[x])
-                send(o_copies[x])
+                target = flip(me_b, x)
+                ba_copy(st_send.at[target], st_recv.at[x - 1], st_sems, x).start()
+                ba_copy(o_send.at[target], o_recv.at[x - 1], o_sems, x).start()
 
     def unpack(packed):
         parts = [packed]
@@ -470,11 +481,9 @@
             parts.append(pltpu.roll(packed, LANES - 2 * heads * g, 1))
         return jnp.concatenate(parts, axis=0)
 
+    take(st_recv, st_sems.at[1])
     tops = []
     for d in range(chips):
-        if d:
-            st_copies[2 * d].wait_recv()
-        st_copies[2 * d + 1].wait_recv()
         mine = st_recv[2 * d - 1] if d else st_send[me_b]
         tops.append(unpack(mine + st_recv[2 * d]))
     overall = tops[0]
@@ -495,12 +504,10 @@
     coarse = shares.astype(BF16)
     fine = (shares - coarse.astype(F32)).astype(BF16)
     wide = dot(coarse, spread) + dot(fine, spread)
+    take(o_recv, o_sems.at[1])
     left = jnp.zeros((own, span), F32)
     right = jnp.zeros((own, span), F32)
     for d in range(chips):
-        if d:
-            o_copies[2 * d].wait_recv()
-        o_copies[2 * d + 1].wait_recv()
         mine = (o_recv[2 * d - 1] if d else o_send[me_b]).astype(F32)
         other = o_recv[2 * d].astype(F32)
         part = wide[d * own : (d + 1) * own]
@@ -508,54 +515,69 @@
         right = right + part[:, span:width] * jnp.where(core == 0, other, mine)
     attended = jnp.concatenate([left, right], axis=1)
     mixed = (attended * gate.astype(F32)).astype(BF16)
-    loads["wo"].wait()
-    tokens_mid = v_tok[...] + dot(mixed, v_wo[...])
+    loaded("wod", v_wod)
+    tokens_mid = v_tok[...] + dot(mixed, v_wod[0:width, :])
     normed_mid = norm(tokens_mid, gains_ref[1:2, :]).astype(BF16)
-    loads["wup"].wait()
+    loaded("wup", v_wup)
     part = 512
     for n in range(0, hidden, part):
         first = dot(normed_mid, v_wup[:, n : n + part])
         second = dot(normed_mid, v_wup[:, hidden + n : hidden + n + part])
         v_inner[:, n : n + part] = (first * jax.nn.sigmoid(first) * second).astype(BF16)
-    loads["wdn"].wait()
-    token_out = tokens_mid + dot(v_inner[...], v_wdn[...])
-    token_round = token_out.astype(BF16)
-    t_own[...] = token_round
-    t_all[me_b] = token_round
-    loads["wta"].wait()
+    outs = []
+    for c in range(2):
+        columns_c = pl.ds(c * span, span)
+        out = dot(v_inner[...], v_wod[width : width + hidden, c * span : (c + 1) * span])
+        out = tokens_mid[:, c * span : (c + 1) * span] + out
+        outs.append(out)
+        t_own[:, columns_c] = out.astype(BF16)
+        t_all[me_b, :, columns_c] = out.astype(BF16)
+        for d in chip_order:
+            ba_copy(
+                t_own.at[:, columns_c], t_all.at[me_b, :, columns_c], t_sems, 2 * d, d
+            ).start()
+    token_out = jnp.concatenate(outs, axis=1)
+    ba_copy(t_own, t_all.at[me_b], tm_sems, 1).start()
+    loaded("wta", v_wta)
     normed_out = norm(token_out, gains_ref[2:3, :]).astype(BF16)
     token_atom = dot(normed_out, v_wta[...]).astype(BF16)
     ta_own[...] = token_atom
     ta_all[me_b] = token_atom
-    ta_copies = {x: ba_copy(ta_own, ta_all.at[me_b], ta_sems, x, x - 1) for x in order}
     for x in order:
-        send(ta_copies[x])
-    t_copies = {
-        d: ba_copy(t_own, t_all.at[me_b], t_sems, 2 * d, d - 1) for d in chip_order
-    }
-    for d in chip_order:
-        send(t_copies[d])
-    tm_copies = {0: ba_copy(t_own, t_all.at[me_b], tm_sems, 1, 0)}
-    send(tm_copies[0])
-    for x in order:
-        ta_copies[x].wait_recv()
+        ba_copy(ta_own, ta_all.at[me_b], ta_sems, x).start()
+    loaded("w_pos_out", w_pos_out_ref)
+    for d in range(1, chips):
+        rows = t_all.at[flip(me_b, 2 * d)]
+        take(rows, t_sems.at[d])
+        ba_copy(rows, rows, tm_sems, 1).start()
+    ta_pieces = ta_all.at[pl.ds(0, n_ba - 1)]
+    take(ta_pieces, ta_sems.at[1])
     picked = dot(v_onehot[...], ta_all[...].reshape(tok_rows, channels))
     atom_normed = norm(v_state[...] + picked, None).astype(BF16)
     update = dot_nt(w_pos_out_ref[...], atom_normed)[:, 0:atoms]
     den_ref[...] = noisy_ref[...] * (inv_scale * inv_scale) + update * (sigma * inv_scale)
-    for d in range(1, chips):
-        piece = flip(me_b, 2 * d)
-        t_copies[d].wait_recv()
-        tm_copies[d] = ba_copy(t_all.at[piece], t_all.at[piece], tm_sems, 1, d)
-        send(tm_copies[d])
-    for d in range(chips):
-        tm_copies[d].wait_recv()
-    for copy in sent:
-        copy.wait_send()
+    t_pieces = t_all.at[pl.ds(0, chips)]
+    take(t_pieces, tm_sems.at[1])
+    for whole, sem in (
+        (state_mate, state_sems),
+        (ids_mate, ids_mate_sems),
+        (ids_all, ids_sems),
+        (sum_recv, sum_sems),
+        (bias_send, bias_sems),
+        (chip_pieces, kvm_sems),
+        (q_pieces, q_sems),
+        (st_recv, st_sems),
+        (o_recv, o_sems),
+        (t_all.at[pl.ds(0, chips - 1)], t_sems),
+        (t_pieces, tm_sems),
+        (ta_pieces, ta_sems),
+    ):
+        take(whole, sem.at[0])
+    take(rows_kv.at[pl.ds(0, n_aa - 1)], kv_send.at[1])
 
     @pl.when(chip != me_a)
     def _():
-        kv_copy(0).wait_send()
+        take(rows_own, kv_send.at[0])
 
 
 def finish_kernel(tok_ref, den_ref, den_out_ref, tok_out_ref):
@@ -592,6 +614,8 @@
     own = tok_rows // n_ba
     chips = n_ba // 2
     half, span, keys_n = heads // 2, width // 2, 2 * cols
+    halves = 2 if own % 32 == 0 else 1
+    half_rows = own // halves
     head_dim = width // heads
     if tok_rows != 2 * cols or chips != n_aa:
         raise ValueError("unsupported mesh")
@@ -634,9 +658,14 @@
             jax.ShapeDtypeStruct((3, atoms), F32),
             jax.ShapeDtypeStruct((n_ba, own, width), BF16),
         ],
-        in_specs=[hbm, vmem, smem, hbm, hbm, hbm, vmem, vmem, vmem] + [hbm] * 7 + [vmem],
+        in_specs=[hbm, hbm, smem] + [hbm] * 14,
         out_specs=[vmem, vmem],
         scratch_shapes=[
+            pltpu.VMEM((3, atoms), F32),
+            pltpu.VMEM(pair_bias_weight.shape, BF16),
+            pltpu.VMEM(gains.shape, F32),
+            pltpu.VMEM(w_pos.shape, F32),
+            pltpu.VMEM(w_pos_out.shape, BF16),
             pltpu.VMEM((atoms_pad, channels), F32),
             pltpu.VMEM((LANES, atoms_pad), F32),
             pltpu.VMEM((atoms_pad, tok_rows), BF16),
@@ -647,18 +676,18 @@
             pltpu.VMEM(w_atom_token.shape, BF16),
             pltpu.VMEM(w_query_gate.shape, BF16),
             pltpu.VMEM((width, width), BF16),
-            pltpu.VMEM(w_attn_out.shape, BF16),
+            pltpu.VMEM((width + w_down.shape[0], width), BF16),
             pltpu.VMEM(w_up.shape, BF16),
-            pltpu.VMEM(w_down.shape, BF16),
             pltpu.VMEM(w_token_atom.shape, BF16),
+            pltpu.VMEM((1, atoms_pad), jnp.int32),
             pltpu.VMEM((1, atoms_pad), jnp.int32),
             pltpu.VMEM((n_ba - 1, 1, atoms_pad), jnp.int32),
             pltpu.VMEM((atoms_pad, channels), BF16),
             pltpu.VMEM((atoms_pad, channels), BF16),
-            pltpu.VMEM((chips, own, width), BF16),
-            pltpu.VMEM((chips - 1, own, width), BF16),
-            pltpu.VMEM((own, width), BF16),
-            pltpu.VMEM((n_ba, own, width), BF16),
+            pltpu.VMEM((halves, chips, half_rows, width), BF16),
+            pltpu.VMEM((halves, chips - 1, half_rows, width), BF16),
+            pltpu.VMEM((halves, half_rows, width), BF16),
+            pltpu.VMEM((n_ba, halves, half_rows, width), BF16),
             pltpu.VMEM((2, own, span), BF16),
             pltpu.VMEM((n_ba, own, span), BF16),
             pltpu.VMEM((half, keys_n, 2 * LANES), BF16),
@@ -672,22 +701,23 @@
             pltpu.VMEM((own, width), BF16),
             pltpu.VMEM((own, channels), BF16),
             pltpu.VMEM((n_ba, own, channels), BF16),
-            dma((11,)),
+            dma((14,)),
             dma((PAIR_CHUNKS,)),
-            dma((2, n_ba - 1)),
-            dma((2, 1)),
-            dma((2, chips - 1)),
-            dma((2, PAIR_CHUNKS)),
-            dma((n_aa,)),
+            dma((2,)),
+            dma((2,)),
+            dma((2,)),
+            dma((1 + halves,)),
+            dma((2,)),
+            dma((2,)),
+            dma((halves, chips)),
+            dma,
+            dma((2,)),
+            dma((2,)),
+            dma((2,)),
+            dma((2,)),
             dma((chips,)),
-            dma,
-            dma((2, chips)),
-            dma((2, n_ba - 1)),
-            dma((2, n_ba - 1)),
-            dma((2, n_ba - 1)),
-            dma((2, chips - 1)),
-            dma((2, chips)),
-            dma((2, n_ba - 1)),
+            dma((2,)),
+            dma((2,)),
         ],
         compiler_params=pltpu.CompilerParams(
             collective_id=0, has_side_effects=True, vmem_limit_bytes=48 * 1024 * 1024

time: 38 us -> 35.6 us (0.937)
  Pallas kernels: 36.5 us -> 34.1 us
    pallas_call x1, Pallas kernels: 35.5 us -> 33.1 us  [on_device(): pl.pallas_call(functools.partial(step_kernel, n_aa, n_ba), out_shape=[jax...]
where the time goes in v3:
time: 35.6 us; the launch traced here: 35.4 us
  Pallas kernels  34.1 us (96%)
  between operations  1.29 us (4%)
    pallas_call x1, Pallas kernels, on_device(): pl.pallas_call(functools.partial(step_kernel, n_aa, n_ba), out_shape=[jax...  33.1 us
    pallas_call x1, Pallas kernels, on_device(): pl.pallas_call(finish_kernel, out_shape=[jax.ShapeDtypeStruct((3, atoms),...  0.93 us

profile of v3, /device:TPU:0, one launch (start us, length us, event | category | flops | bytes accessed | tf_op | source)
XLA Modules:
  0.0 35.4 jit_solution(6960497218209642571)
XLA Ops:
  1.3 33.1 %shard_map.176 = (f32[3,384]{1,0:T(4,128)S(1)}, bf16[8,32,768]{2,1,0:T(8,128)(2,1)S(1)}) custom-call(f32[384,128]{1,0:T(8,128)} %atom_hbm.1, f32[3,384]{1,0:T(4,128)} %noisy_hbm.1, f32[1]{0:T(128)S(6)} %copy.19.noise_ref, s32[384]{0:T(512)} %ids_hbm.1, f32[256,768]{1,0:T(8,128)} %tok_hbm.1, bf16[256,128,128]{2,1,0:T(8,128)(2,1)} %pair_hbm.1, ...), custom_call_target="tpu_custom_call" | custom-call | tf_op jit(solution)/shard_map/pallas_call | solution.py:655
  34.4 0.9 %shard_map.177 = (f32[3,384]{1,0:T(4,128)}, f32[256,768]{1,0:T(8,128)}) custom-call(bf16[256,768]{1,0:T(8,128)(2,1)S(1)} %bitcast.1, f32[3,384]{1,0:T(4,128)S(1)} %get-tuple-element.5.den_ref), custom_call_target="tpu_custom_call" | custom-call | tf_op jit(solution)/shard_map/pallas_call | solution.py:726

commit v4 on v3

--- a/solution.py
+++ b/solution.py
@@ -11,8 +11,8 @@
 F32 = jnp.float32
 BF16 = jnp.bfloat16
 LANES = 128
-PAIR_CHUNKS = 4
-EARLY_CHUNKS = 2
+PAIR_CHUNKS = 8
+EARLY_CHUNKS = 3
 BIAS_ROWS = 8
 
 
@@ -117,7 +117,6 @@
     bias_sems,
     kv_send,
     kv_recv,
-    kv_local,
     kvm_sems,
     q_sems,
     o_sems,
@@ -135,7 +134,7 @@
     head_dim = width // heads
     span = width // 2
     hidden = v_wod.shape[0] - width
-    halves, half_rows = rows_own.shape[:2]
+    parts, part_rows = rows_own.shape[:2]
     chips = n_ba // 2
     keys_n = 2 * cols
     me_a = lax.axis_index("aa")
@@ -199,17 +198,17 @@
     barrier = pltpu.get_barrier_semaphore()
     for x in range(1, n_ba):
         greet(at(me_a, flip(me_b, x)))
+    block = me_b // chips
+    column = 2 * me_a + block
     for x in range(1, n_aa):
-        greet(at(flip(me_a, x), 2 * me_a + core))
-    for x in range(1, chips):
-        greet(at(chip, flip(me_b, 2 * x)))
+        greet(at(flip(me_a, x), column))
 
     @pl.when(chip != me_a)
     def _():
-        greet(at(me_a, 2 * me_a + core))
-        greet(at(chip, me_b))
-
-    greetings = n_ba - 1 + n_aa - 1 + chips - 1 + jnp.where(chip != me_a, 2, 0)
+        for j in range(chips):
+            greet(at(chip, core * chips + j))
+
+    greetings = n_ba - 1 + n_aa - 1 + jnp.where(chip != me_a, chips, 0)
 
     for name in names[5:8]:
         load(name)
@@ -259,30 +258,37 @@
     for x in order:
         ba_copy(v_ids, ids_all.at[x - 1], ids_sems, x).start()
 
-    def select(ids, part):
-        row = lax.broadcasted_iota(jnp.int32, (chips * half_rows, atoms_pad), 0)
-        token = lax.rem(row, half_rows) + 2 * own * (row // half_rows)
-        token = token + (own * core + me_a * tok_rows + part * half_rows)
+    group = max(1, parts // 2)
+
+    def select(ids, first):
+        row = lax.broadcasted_iota(jnp.int32, (group * chips * part_rows, atoms_pad), 0)
+        token = lax.rem(row, part_rows) + 2 * own * lax.rem(row // part_rows, chips)
+        token = token + part_rows * (first + row // (part_rows * chips))
+        token = token + (own * core + me_a * tok_rows)
         return jnp.where(token == ids, 1.0, 0.0).astype(BF16)
 
     loaded("wat", v_wat)
     hidden_own = jnp.maximum(dot(rounded, v_wat[...]), 0.0).astype(BF16)
-    own_sums = [dot(select(ids_row, part), hidden_own) for part in range(halves)]
+    firsts = range(0, parts, group)
+    own_sums = [dot(select(ids_row, first), hidden_own) for first in firsts]
     take(ids_mate, ids_mate_sems.at[1])
-    selectors = [select(ids_mate[...], part) for part in range(halves)]
+    selectors = [select(ids_mate[...], first) for first in firsts]
     take(state_mate, state_sems.at[1])
     hidden_mate = jnp.maximum(dot(state_mate[...], v_wat[...]), 0.0).astype(BF16)
-    for part in range(halves):
-        chip_sums = own_sums[part] + dot(selectors[part], hidden_mate)
-        sum_send[part] = chip_sums.astype(BF16).reshape(chips, half_rows, width)
-        for d in chip_order:
-            ba_copy(
-                sum_send.at[part, flip(chip, d)],
-                sum_recv.at[part, d - 1],
-                sum_sems,
-                2 * d,
-                1 + part,
-            ).start()
+    for first, sums, selector in zip(firsts, own_sums, selectors):
+        chip_sums = sums + dot(selector, hidden_mate)
+        sum_send[first : first + group] = chip_sums.astype(BF16).reshape(
+            group, chips, part_rows, width
+        )
+        for part in range(first, first + group):
+            for d in chip_order:
+                ba_copy(
+                    sum_send.at[part, flip(chip, d)],
+                    sum_recv.at[part, d - 1],
+                    sum_sems,
+                    2 * d,
+                    1 + part,
+                ).start()
 
     lane_id = lax.broadcasted_iota(jnp.int32, (atoms_pad, tok_rows), 1) + me_a * tok_rows
     v_onehot[...] = jnp.where(columns[:, 3:4] == lane_id.astype(F32), 1.0, 0.0).astype(BF16)
@@ -337,38 +343,41 @@
     loaded("tok", v_tok)
     loaded("gains", gains_ref)
 
+    slot = lax.rem(me_b, chips)
+
     def kv_copy(x, part):
         return pltpu.make_async_remote_copy(
             src_ref=rows_own.at[part],
             dst_ref=rows_kv.at[me_b, part],
             send_sem=kv_send.at[1 if x else 0],
-            recv_sem=kv_recv.at[part, chip],
-            device_id=at(flip(me_a, x), 2 * me_a + core),
+            recv_sem=kv_recv.at[part, slot],
+            device_id=at(flip(me_a, x), column),
             device_id_type=MESH,
         )
 
-    own_piece = pltpu.make_async_copy(rows_own, rows_kv.at[me_b], kv_local)
-    for part in range(halves):
-        rows = pl.ds(part * half_rows, half_rows)
+    for part in range(parts):
+        rows = pl.ds(part * part_rows, part_rows)
         summed = sum_send[part, chip].astype(F32)
         take(sum_recv.at[part], sum_sems.at[1 + part])
         for d in chip_order:
             summed = summed + sum_recv[part, d - 1].astype(F32)
         tokens_start = (
-            v_tok[rows, :] + summed / counts[part * half_rows : (part + 1) * half_rows]
+            v_tok[rows, :] + summed / counts[part * part_rows : (part + 1) * part_rows]
         )
         v_tok[rows, :] = tokens_start
         rows_own[part] = norm(tokens_start, gains_ref[0:1, :]).astype(BF16)
-        for x in far_first(n_aa):
+        for x in range(n_aa - 1, 0, -1):
             kv_copy(x, part).start()
 
-        @pl.when(chip != me_a)
+        @pl.when(column != me_b)
         def _():
             kv_copy(0, part).start()
 
-    @pl.when(chip == me_a)
-    def _():
-        own_piece.start()
+        @pl.when(column == me_b)
+        def _():
+            pltpu.make_async_copy(
+                rows_own.at[part], rows_kv.at[me_b, part], kv_recv.at[part, slot]
+            ).start()
 
     normed = rows_own[...].reshape(own, width)
     loaded("wqg", v_wqg)
@@ -382,50 +391,40 @@
 
     for c in range(EARLY_CHUNKS, PAIR_CHUNKS):
         bias_chunk(c)
-
-    @pl.when(chip == me_a)
-    def _():
-        own_piece.wait()
-
-    for part in range(halves):
-        for d in range(chips):
-            piece = flip(me_b, 2 * d)
-            rows = rows_kv.at[piece, part]
-            arrival = kv_recv.at[part, flip(chip, d)]
-            if d:
-                take(rows, arrival)
-            else:
-
-                @pl.when(chip != me_a)
-                def _():
-                    take(rows, arrival)
-
+    for part in range(parts):
+        for j in range(chips):
+            rows = rows_kv.at[core * chips + j, part]
+            take(rows, kv_recv.at[part, j])
             ba_copy(rows, rows, kvm_sems, 1).start()
     loaded("wkv", v_wkv)
     chip_pieces = rows_kv.at[pl.ds(0, chips)]
-    take(chip_pieces, kvm_sems.at[1])
-
-    key_value = dot(rows_kv[...].reshape(keys_n, width), v_wkv[...])
     spans = []
     for h in range(half):
         lo = h * head_dim // LANES * LANES
         hi = ((h + 1) * head_dim + LANES - 1) // LANES * LANES
         spans.append((lo, hi))
-        lane = lax.broadcasted_iota(jnp.int32, (keys_n, hi - lo), 1) + lo
-        mine = (lane >= h * head_dim) & (lane < (h + 1) * head_dim)
-        v_km[h, :, 0 : hi - lo] = jnp.where(mine, key_value[:, lo:hi], 0.0).astype(BF16)
     tiles = []
     for t in range(span // LANES):
-        h0 = t * LANES // head_dim
-        h1 = (t * LANES + LANES - 1) // head_dim
-        tiles.append((h0, h1))
-        part = key_value[:, span + t * LANES : span + (t + 1) * LANES]
-        lane = lax.broadcasted_iota(jnp.int32, (keys_n, LANES), 1) + t * LANES
-        for h in range(h0, h1 + 1):
+        tiles.append((t * LANES // head_dim, (t * LANES + LANES - 1) // head_dim))
+
+    def project(which):
+        pieces = rows_kv[pl.ds(which * chips, chips)].reshape(cols, width)
+        key_value = dot(pieces, v_wkv[...])
+        keys = pl.ds(pl.multiple_of(which * cols, cols), cols)
+        for h, (lo, hi) in enumerate(spans):
+            lane = lax.broadcasted_iota(jnp.int32, (cols, hi - lo), 1) + lo
             mine = (lane >= h * head_dim) & (lane < (h + 1) * head_dim)
-            v_vm[t, (h - h0) * keys_n : (h - h0 + 1) * keys_n, :] = jnp.where(
-                mine, part, 0.0
-            ).astype(BF16)
+            v_km[h, keys, 0 : hi - lo] = jnp.where(mine, key_value[:, lo:hi], 0.0).astype(BF16)
+        for t, (h0, h1) in enumerate(tiles):
+            piece = key_value[:, span + t * LANES : span + (t + 1) * LANES]
+            lane = lax.broadcasted_iota(jnp.int32, (cols, LANES), 1) + t * LANES
+            for h in range(h0, h1 + 1):
+                mine = (lane >= h * head_dim) & (lane < (h + 1) * head_dim)
+                v_vm[t, h - h0, keys, :] = jnp.where(mine, piece, 0.0).astype(BF16)
+
+    project(core)
+    take(chip_pieces, kvm_sems.at[1])
+    project(1 - core)
 
     q_pieces = q_all.at[pl.ds(0, n_ba - 1)]
     take(q_pieces, q_sems.at[1])
@@ -433,47 +432,65 @@
 
     scale = head_dim ** (-0.5)
     rows2 = 2 * own
-    lane = lax.broadcasted_iota(jnp.int32, (rows2, LANES), 1)
-    top_lane = lane - half * core
+    batches = [chip_order[:2]] + [[d] for d in chip_order[2:]] + [[0]]
     groups = own // 8
-    for d in chip_order + [0]:
-        duo = flip(chip, d)
-        stats = jnp.zeros((rows2, LANES), F32)
-        q_rows = q_all[pl.ds(2 * duo, 2)].reshape(rows2, span)
+    for duos in batches:
+        places = [flip(chip, d) for d in duos]
+        many = len(places)
+        lane = lax.broadcasted_iota(jnp.int32, (many * rows2, LANES), 1)
+        top_lane = lane - half * core
+        stats = jnp.zeros((many * rows2, LANES), F32)
+        q_rows = jnp.concatenate(
+            [q_all[pl.ds(2 * duo, 2)].reshape(rows2, span) for duo in places], axis=0
+        )
         for h in range(half):
             lo, hi = spans[h]
             scores = dot_nt(q_rows[:, lo:hi], v_km[h, :, 0 : hi - lo]) * scale
-            where = pl.ds(duo * (rows2 * half) + h, rows2, stride=half)
-            parts = [
-                scores[:, k * cols : (k + 1) * cols] + v_bias[k, where, :] for k in range(2)
+            pair_bias = [
+                jnp.concatenate(
+                    [
+                        v_bias[k, pl.ds(duo * (rows2 * half) + h, rows2, stride=half), :]
+                        for duo in places
+                    ],
+                    axis=0,
+                )
+                for k in range(2)
             ]
-            top = jnp.max(jnp.maximum(parts[0], parts[1]), axis=1, keepdims=True)
-            parts = [jnp.exp(part - top) for part in parts]
-            total = jnp.sum(parts[0] + parts[1], axis=1, keepdims=True)
+            both = [scores[:, k * cols : (k + 1) * cols] + pair_bias[k] for k in range(2)]
+            top = jnp.max(jnp.maximum(both[0], both[1]), axis=1, keepdims=True)
+            both = [jnp.exp(one - top) for one in both]
+            total = jnp.sum(both[0] + both[1], axis=1, keepdims=True)
             stats = jnp.where(top_lane == h, top, stats)
             stats = jnp.where(top_lane == heads + h, total, stats)
             for k in range(2):
-                v_p[:, h * keys_n + k * cols : h * keys_n + (k + 1) * cols] = parts[k].astype(
-                    BF16
-                )
+                v_p[0 : many * rows2, h * keys_n + k * cols : h * keys_n + (k + 1) * cols] = both[k].astype(BF16)
         for t, (h0, h1) in enumerate(tiles):
+            count = (h1 - h0 + 1) * keys_n
             out = dot(
-                v_p[:, h0 * keys_n : (h1 + 1) * keys_n], v_vm[t, 0 : (h1 - h0 + 1) * keys_n, :]
-            )
-            o_send[pl.ds(2 * duo, 2), :, t * LANES : (t + 1) * LANES] = out.astype(BF16).reshape(
-                2, own, LANES
-            )
-        for c in range(2):
-            packed = stats[c * own : c * own + 8]
-            for g in range(1, groups):
-                piece = pltpu.roll(stats[c * own + 8 * g : c * own + 8 * g + 8], 2 * heads * g, 1)
-                packed = jnp.where(lane[0:8] >= 2 * heads * g, piece, packed)
-            st_send[2 * duo + c] = packed
-        for x in (2 * d + 1, 2 * d):
-            if x:
-                target = flip(me_b, x)
-                ba_copy(st_send.at[target], st_recv.at[x - 1], st_sems, x).start()
-                ba_copy(o_send.at[target], o_recv.at[x - 1], o_sems, x).start()
+                v_p[0 : many * rows2, h0 * keys_n : h0 * keys_n + count],
+                v_vm[t, 0 : h1 - h0 + 1].reshape(count, LANES),
+            ).astype(BF16)
+            for i, duo in enumerate(places):
+                o_send[pl.ds(2 * duo, 2), :, t * LANES : (t + 1) * LANES] = out[
+                    i * rows2 : (i + 1) * rows2
+                ].reshape(2, own, LANES)
+        for i, duo in enumerate(places):
+            for c in range(2):
+                at_row = i * rows2 + c * own
+                packed = stats[at_row : at_row + 8]
+                for g in range(1, groups):
+                    piece = stats[at_row + 8 * g : at_row + 8 * g + 8]
+                    piece = pltpu.roll(piece, 2 * heads * g, 1)
+                    packed = jnp.where(lane[0:8] >= 2 * heads * g, piece, packed)
+                st_send[2 * duo + c] = packed
+        for d in duos:
+            for x in (2 * d + 1, 2 * d):
+                if x:
+                    target = flip(me_b, x)
+                    ba_copy(st_send.at[target], st_recv.at[x - 1], st_sems, x).start()
+                    ba_copy(o_send.at[target], o_recv.at[x - 1], o_sems, x).start()
+
+    lane = lax.broadcasted_iota(jnp.int32, (own, LANES), 1)
 
     def unpack(packed):
         parts = [packed]
@@ -497,7 +514,7 @@
     head_lane = lax.broadcasted_iota(jnp.int32, (LANES, width), 1)
     inside = (head_lane >= head_row * head_dim) & (head_lane < (head_row + 1) * head_dim)
     spread = jnp.where(inside, 1.0, 0.0).astype(BF16)
-    live = lane[0:own] < heads
+    live = lane < heads
     shares = jnp.concatenate(
         [jnp.where(live, factor / denominator, 0.0) for factor in factors], axis=0
     )
@@ -525,19 +542,23 @@
         second = dot(normed_mid, v_wup[:, hidden + n : hidden + n + part])
         v_inner[:, n : n + part] = (first * jax.nn.sigmoid(first) * second).astype(BF16)
     outs = []
-    for c in range(2):
+
+    def share(c):
         columns_c = pl.ds(c * span, span)
-        out = dot(v_inner[...], v_wod[width : width + hidden, c * span : (c + 1) * span])
-        out = tokens_mid[:, c * span : (c + 1) * span] + out
-        outs.append(out)
-        t_own[:, columns_c] = out.astype(BF16)
-        t_all[me_b, :, columns_c] = out.astype(BF16)
         for d in chip_order:
             ba_copy(
                 t_own.at[:, columns_c], t_all.at[me_b, :, columns_c], t_sems, 2 * d, d
             ).start()
+
+    for c in range(2):
+        out = dot(v_inner[...], v_wod[width : width + hidden, c * span : (c + 1) * span])
+        out = tokens_mid[:, c * span : (c + 1) * span] + out
+        outs.append(out)
+        t_own[:, c * span : (c + 1) * span] = out.astype(BF16)
+        t_all[me_b, :, c * span : (c + 1) * span] = out.astype(BF16)
+        if c == 0:
+            share(0)
     token_out = jnp.concatenate(outs, axis=1)
-    ba_copy(t_own, t_all.at[me_b], tm_sems, 1).start()
     loaded("wta", v_wta)
     normed_out = norm(token_out, gains_ref[2:3, :]).astype(BF16)
     token_atom = dot(normed_out, v_wta[...]).astype(BF16)
@@ -545,13 +566,15 @@
     ta_all[me_b] = token_atom
     for x in order:
         ba_copy(ta_own, ta_all.at[me_b], ta_sems, x).start()
+    share(1)
+    ba_copy(t_own, t_all.at[me_b], tm_sems, 1).start()
     loaded("w_pos_out", w_pos_out_ref)
+    ta_pieces = ta_all.at[pl.ds(0, n_ba - 1)]
+    take(ta_pieces, ta_sems.at[1])
     for d in range(1, chips):
         rows = t_all.at[flip(me_b, 2 * d)]
         take(rows, t_sems.at[d])
         ba_copy(rows, rows, tm_sems, 1).start()
-    ta_pieces = ta_all.at[pl.ds(0, n_ba - 1)]
-    take(ta_pieces, ta_sems.at[1])
     picked = dot(v_onehot[...], ta_all[...].reshape(tok_rows, channels))
     atom_normed = norm(v_state[...] + picked, None).astype(BF16)
     update = dot_nt(w_pos_out_ref[...], atom_normed)[:, 0:atoms]
@@ -575,7 +598,7 @@
         take(whole, sem.at[0])
     take(rows_kv.at[pl.ds(0, n_aa - 1)], kv_send.at[1])
 
-    @pl.when(chip != me_a)
+    @pl.when(column != me_b)
     def _():
         take(rows_own, kv_send.at[0])
 
@@ -614,8 +637,8 @@
     own = tok_rows // n_ba
     chips = n_ba // 2
     half, span, keys_n = heads // 2, width // 2, 2 * cols
-    halves = 2 if own % 32 == 0 else 1
-    half_rows = own // halves
+    part_rows = 8
+    parts = own // part_rows
     head_dim = width // heads
     if tok_rows != 2 * cols or chips != n_aa:
         raise ValueError("unsupported mesh")
@@ -684,15 +707,15 @@
             pltpu.VMEM((n_ba - 1, 1, atoms_pad), jnp.int32),
             pltpu.VMEM((atoms_pad, channels), BF16),
             pltpu.VMEM((atoms_pad, channels), BF16),
-            pltpu.VMEM((halves, chips, half_rows, width), BF16),
-            pltpu.VMEM((halves, chips - 1, half_rows, width), BF16),
-            pltpu.VMEM((halves, half_rows, width), BF16),
-            pltpu.VMEM((n_ba, halves, half_rows, width), BF16),
+            pltpu.VMEM((parts, chips, part_rows, width), BF16),
+            pltpu.VMEM((parts, chips - 1, part_rows, width), BF16),
+            pltpu.VMEM((parts, part_rows, width), BF16),
+            pltpu.VMEM((n_ba, parts, part_rows, width), BF16),
             pltpu.VMEM((2, own, span), BF16),
             pltpu.VMEM((n_ba, own, span), BF16),
             pltpu.VMEM((half, keys_n, 2 * LANES), BF16),
-            pltpu.VMEM((span // LANES, tile_heads * keys_n, LANES), BF16),
-            pltpu.VMEM((2 * own, half * keys_n), BF16),
+            pltpu.VMEM((span // LANES, tile_heads, keys_n, LANES), BF16),
+            pltpu.VMEM((4 * own, half * keys_n), BF16),
             pltpu.VMEM((n_ba, own, span), BF16),
             pltpu.VMEM((n_ba - 1, own, span), BF16),
             pltpu.VMEM((n_ba, 8, LANES), F32),
@@ -706,11 +729,10 @@
             dma((2,)),
             dma((2,)),
             dma((2,)),
-            dma((1 + halves,)),
-            dma((2,)),
-            dma((2,)),
-            dma((halves, chips)),
-            dma,
+            dma((1 + parts,)),
+            dma((2,)),
+            dma((2,)),
+            dma((parts, chips)),
             dma((2,)),
             dma((2,)),
             dma((2,)),

time: 35.6 us -> 35.2 us (0.989)
  Pallas kernels: 34.1 us -> 33.7 us
    pallas_call x1, Pallas kernels: 33.1 us -> 32.7 us  [on_device(): pl.pallas_call(functools.partial(step_kernel, n_aa, n_ba), out_shape=[jax...]
where the time goes in v4:
time: 35.2 us; the launch traced here: 35 us
  Pallas kernels  33.7 us (96%)
  between operations  1.29 us (4%)
    pallas_call x1, Pallas kernels, on_device(): pl.pallas_call(functools.partial(step_kernel, n_aa, n_ba), out_shape=[jax...  32.7 us
    pallas_call x1, Pallas kernels, on_device(): pl.pallas_call(finish_kernel, out_shape=[jax.ShapeDtypeStruct((3, atoms),...  0.93 us

profile of v4, /device:TPU:0, one launch (start us, length us, event | category | flops | bytes accessed | tf_op | source)
XLA Modules:
  0.0 35.0 jit_solution(16203982095019700374)
XLA Ops:
  1.3 32.7 %shard_map.176 = (f32[3,384]{1,0:T(4,128)S(1)}, bf16[8,32,768]{2,1,0:T(8,128)(2,1)S(1)}) custom-call(f32[384,128]{1,0:T(8,128)} %atom_hbm.1, f32[3,384]{1,0:T(4,128)} %noisy_hbm.1, f32[1]{0:T(128)S(6)} %copy.19.noise_ref, s32[384]{0:T(512)} %ids_hbm.1, f32[256,768]{1,0:T(8,128)} %tok_hbm.1, bf16[256,128,128]{2,1,0:T(8,128)(2,1)} %pair_hbm.1, ...), custom_call_target="tpu_custom_call" | custom-call | tf_op jit(solution)/shard_map/pallas_call | solution.py:678
  34.0 0.9 %shard_map.177 = (f32[3,384]{1,0:T(4,128)}, f32[256,768]{1,0:T(8,128)}) custom-call(bf16[256,768]{1,0:T(8,128)(2,1)S(1)} %bitcast.1, f32[3,384]{1,0:T(4,128)S(1)} %get-tuple-element.5.den_ref), custom_call_target="tpu_custom_call" | custom-call | tf_op jit(solution)/shard_map/pallas_call | solution.py:748

commit v5 on v4

--- a/solution.py
+++ b/solution.py
@@ -182,9 +182,11 @@
     step = tok_rows // PAIR_CHUNKS
     pair_loads = [
         pltpu.make_async_copy(
-            pair_hbm.at[pl.ds(c * step, step)], v_pair.at[pl.ds(c * step, step)], pair_sem.at[c]
-        )
-        for c in range(PAIR_CHUNKS)
+            pair_hbm.at[pl.ds(c * step, 2 * step)],
+            v_pair.at[pl.ds(c * step, 2 * step)],
+            pair_sem.at[c // 2],
+        )
+        for c in range(0, PAIR_CHUNKS, 2)
     ]
     for name in names[:5]:
         load(name)
@@ -257,7 +259,6 @@
     ba_copy(v_ids, ids_mate, ids_mate_sems, 1).start()
     for x in order:
         ba_copy(v_ids, ids_all.at[x - 1], ids_sems, x).start()
-
     group = max(1, parts // 2)
 
     def select(ids, first):
@@ -314,7 +315,8 @@
     ]
 
     def bias_chunk(c):
-        pair_loads[c].wait()
+        if c % 2 == 0:
+            pair_loads[c // 2].wait()
 
         def rows(r, carry):
             start = c * step + r * BIAS_ROWS
@@ -343,15 +345,22 @@
     loaded("tok", v_tok)
     loaded("gains", gains_ref)
 
-    slot = lax.rem(me_b, chips)
-
-    def kv_copy(x, part):
+    low = jnp.where(2 * me_a < n_aa, me_a, n_aa - 1 - me_a)
+
+    def plane(k):
+        if k < 0:
+            return me_a
+        place = n_aa - 1 - k
+        place = jnp.where(place > low, place, k - (n_aa - 1 - low))
+        return jnp.where(2 * me_a < n_aa, place, n_aa - 1 - place)
+
+    def kv_copy(k, part):
         return pltpu.make_async_remote_copy(
             src_ref=rows_own.at[part],
             dst_ref=rows_kv.at[me_b, part],
-            send_sem=kv_send.at[1 if x else 0],
-            recv_sem=kv_recv.at[part, slot],
-            device_id=at(flip(me_a, x), column),
+            send_sem=kv_send.at[1 if k >= 0 else 0],
+            recv_sem=kv_recv.at[part],
+            device_id=at(plane(k), column),
             device_id_type=MESH,
         )
 
@@ -366,17 +375,17 @@
         )
         v_tok[rows, :] = tokens_start
         rows_own[part] = norm(tokens_start, gains_ref[0:1, :]).astype(BF16)
-        for x in range(n_aa - 1, 0, -1):
-            kv_copy(x, part).start()
+        for k in range(n_aa - 1):
+            kv_copy(k, part).start()
 
         @pl.when(column != me_b)
         def _():
-            kv_copy(0, part).start()
+            kv_copy(-1, part).start()
 
         @pl.when(column == me_b)
         def _():
             pltpu.make_async_copy(
-                rows_own.at[part], rows_kv.at[me_b, part], kv_recv.at[part, slot]
+                rows_own.at[part], rows_kv.at[me_b, part], kv_recv.at[part]
             ).start()
 
     normed = rows_own[...].reshape(own, width)
@@ -385,17 +394,17 @@
     for c in range(2):
         q_own[c] = query[:, c * span : (c + 1) * span]
     q_all[me_b] = q_own[core]
-    for x in order:
-        ba_copy(q_own.at[lax.rem(core + x, 2)], q_all.at[me_b], q_sems, x).start()
     gate = jax.nn.sigmoid(dot(normed, v_wqg[:, width : 2 * width])).astype(BF16)
 
     for c in range(EARLY_CHUNKS, PAIR_CHUNKS):
         bias_chunk(c)
+        if c == EARLY_CHUNKS + 1:
+            for x in order:
+                ba_copy(q_own.at[lax.rem(core + x, 2)], q_all.at[me_b], q_sems, x).start()
     for part in range(parts):
-        for j in range(chips):
-            rows = rows_kv.at[core * chips + j, part]
-            take(rows, kv_recv.at[part, j])
-            ba_copy(rows, rows, kvm_sems, 1).start()
+        rows = rows_kv.at[pl.ds(core * chips, chips), part]
+        take(rows, kv_recv.at[part])
+        ba_copy(rows, rows, kvm_sems, 1).start()
     loaded("wkv", v_wkv)
     chip_pieces = rows_kv.at[pl.ds(0, chips)]
     spans = []
@@ -411,10 +420,16 @@
         pieces = rows_kv[pl.ds(which * chips, chips)].reshape(cols, width)
         key_value = dot(pieces, v_wkv[...])
         keys = pl.ds(pl.multiple_of(which * cols, cols), cols)
+        turned = [
+            key_value[:, t * LANES : (t + 1) * LANES].T for t in range(span // LANES)
+        ]
         for h, (lo, hi) in enumerate(spans):
-            lane = lax.broadcasted_iota(jnp.int32, (cols, hi - lo), 1) + lo
-            mine = (lane >= h * head_dim) & (lane < (h + 1) * head_dim)
-            v_km[h, keys, 0 : hi - lo] = jnp.where(mine, key_value[:, lo:hi], 0.0).astype(BF16)
+            for t in range(lo // LANES, hi // LANES):
+                row = lax.broadcasted_iota(jnp.int32, (LANES, cols), 0) + t * LANES
+                mine = (row >= h * head_dim) & (row < (h + 1) * head_dim)
+                v_km[h, t * LANES - lo : (t + 1) * LANES - lo, keys] = jnp.where(
+                    mine, turned[t], 0.0
+                ).astype(BF16)
         for t, (h0, h1) in enumerate(tiles):
             piece = key_value[:, span + t * LANES : span + (t + 1) * LANES]
             lane = lax.broadcasted_iota(jnp.int32, (cols, LANES), 1) + t * LANES
@@ -432,7 +447,7 @@
 
     scale = head_dim ** (-0.5)
     rows2 = 2 * own
-    batches = [chip_order[:2]] + [[d] for d in chip_order[2:]] + [[0]]
+    batches = [chip_order[:1]] + [chip_order[n : n + 2] for n in range(1, chips - 1, 2)] + [[0]]
     groups = own // 8
     for duos in batches:
         places = [flip(chip, d) for d in duos]
@@ -445,7 +460,7 @@
         )
         for h in range(half):
             lo, hi = spans[h]
-            scores = dot_nt(q_rows[:, lo:hi], v_km[h, :, 0 : hi - lo]) * scale
+            scores = dot(q_rows[:, lo:hi], v_km[h, 0 : hi - lo, :]) * scale
             pair_bias = [
                 jnp.concatenate(
                     [
@@ -547,7 +562,11 @@
         columns_c = pl.ds(c * span, span)
         for d in chip_order:
             ba_copy(
-                t_own.at[:, columns_c], t_all.at[me_b, :, columns_c], t_sems, 2 * d, d
+                t_own.at[:, columns_c],
+                t_all.at[me_b, :, columns_c],
+                t_sems,
+                2 * d,
+                c * (chips - 1) + d,
             ).start()
 
     for c in range(2):
@@ -569,12 +588,13 @@
     share(1)
     ba_copy(t_own, t_all.at[me_b], tm_sems, 1).start()
     loaded("w_pos_out", w_pos_out_ref)
+    for c in range(2):
+        for d in range(1, chips):
+            rows = t_all.at[flip(me_b, 2 * d), :, pl.ds(c * span, span)]
+            take(rows, t_sems.at[c * (chips - 1) + d])
+            ba_copy(rows, rows, tm_sems, 1).start()
     ta_pieces = ta_all.at[pl.ds(0, n_ba - 1)]
     take(ta_pieces, ta_sems.at[1])
-    for d in range(1, chips):
-        rows = t_all.at[flip(me_b, 2 * d)]
-        take(rows, t_sems.at[d])
-        ba_copy(rows, rows, tm_sems, 1).start()
     picked = dot(v_onehot[...], ta_all[...].reshape(tok_rows, channels))
     atom_normed = norm(v_state[...] + picked, None).astype(BF16)
     update = dot_nt(w_pos_out_ref[...], atom_normed)[:, 0:atoms]
@@ -637,7 +657,7 @@
     own = tok_rows // n_ba
     chips = n_ba // 2
     half, span, keys_n = heads // 2, width // 2, 2 * cols
-    part_rows = 8
+    part_rows = min(16, own)
     parts = own // part_rows
     head_dim = width // heads
     if tok_rows != 2 * cols or chips != n_aa:
@@ -713,7 +733,7 @@
             pltpu.VMEM((n_ba, parts, part_rows, width), BF16),
             pltpu.VMEM((2, own, span), BF16),
             pltpu.VMEM((n_ba, own, span), BF16),
-            pltpu.VMEM((half, keys_n, 2 * LANES), BF16),
+            pltpu.VMEM((half, 2 * LANES, keys_n), BF16),
             pltpu.VMEM((span // LANES, tile_heads, keys_n, LANES), BF16),
             pltpu.VMEM((4 * own, half * keys_n), BF16),
             pltpu.VMEM((n_ba, own, span), BF16),
@@ -725,19 +745,19 @@
             pltpu.VMEM((own, channels), BF16),
             pltpu.VMEM((n_ba, own, channels), BF16),
             dma((14,)),
-            dma((PAIR_CHUNKS,)),
+            dma((PAIR_CHUNKS // 2,)),
             dma((2,)),
             dma((2,)),
             dma((2,)),
             dma((1 + parts,)),
             dma((2,)),
             dma((2,)),
-            dma((parts, chips)),
-            dma((2,)),
-            dma((2,)),
-            dma((2,)),
-            dma((2,)),
-            dma((chips,)),
+            dma((parts,)),
+            dma((2,)),
+            dma((2,)),
+            dma((2,)),
+            dma((2,)),
+            dma((2 * chips - 1,)),
             dma((2,)),
             dma((2,)),
         ],

time: 35.2 us -> 34.9 us (level)
  no operation moved by 1% of the time
where the time goes in v5:
time: 34.9 us; the launch traced here: 34.7 us
  Pallas kernels  33.4 us (96%)
  between operations  1.29 us (4%)
    pallas_call x1, Pallas kernels, on_device(): pl.pallas_call(functools.partial(step_kernel, n_aa, n_ba), out_shape=[jax...  32.5 us
    pallas_call x1, Pallas kernels, on_device(): pl.pallas_call(finish_kernel, out_shape=[jax.ShapeDtypeStruct((3, atoms),...  0.93 us

profile of v5, /device:TPU:0, one launch (start us, length us, event | category | flops | bytes accessed | tf_op | source)
XLA Modules:
  0.0 34.7 jit_solution(9953283177469211086)
XLA Ops:
  1.3 32.5 %shard_map.176 = (f32[3,384]{1,0:T(4,128)S(1)}, bf16[8,32,768]{2,1,0:T(8,128)(2,1)S(1)}) custom-call(f32[384,128]{1,0:T(8,128)} %atom_hbm.1, f32[3,384]{1,0:T(4,128)} %noisy_hbm.1, f32[1]{0:T(128)S(6)} %copy.19.noise_ref, s32[384]{0:T(512)} %ids_hbm.1, f32[256,768]{1,0:T(8,128)} %tok_hbm.1, bf16[256,128,128]{2,1,0:T(8,128)(2,1)} %pair_hbm.1, ...), custom_call_target="tpu_custom_call" | custom-call | tf_op jit(solution)/shard_map/pallas_call | solution.py:698
  33.8 0.9 %shard_map.177 = (f32[3,384]{1,0:T(4,128)}, f32[256,768]{1,0:T(8,128)}) custom-call(bf16[256,768]{1,0:T(8,128)(2,1)S(1)} %bitcast.1, f32[3,384]{1,0:T(4,128)S(1)} %get-tuple-element.5.den_ref), custom_call_target="tpu_custom_call" | custom-call | tf_op jit(solution)/shard_map/pallas_call | solution.py:768

commit v6 on v5

--- a/solution.py
+++ b/solution.py
@@ -657,7 +657,7 @@
     own = tok_rows // n_ba
     chips = n_ba // 2
     half, span, keys_n = heads // 2, width // 2, 2 * cols
-    part_rows = min(16, own)
+    part_rows = 8
     parts = own // part_rows
     head_dim = width // heads
     if tok_rows != 2 * cols or chips != n_aa:

time: 34.9 us -> 34.5 us (0.989)
  Pallas kernels: 33.4 us -> 33 us
    pallas_call x1, Pallas kernels: 32.5 us -> 32.1 us  [on_device(): pl.pallas_call(functools.partial(step_kernel, n_aa, n_ba), out_shape=[jax...]
where the time goes in v6:
time: 34.5 us; the launch traced here: 34.3 us
  Pallas kernels  33 us (96%)
  between operations  1.29 us (4%)
    pallas_call x1, Pallas kernels, on_device(): pl.pallas_call(functools.partial(step_kernel, n_aa, n_ba), out_shape=[jax...  32.1 us
    pallas_call x1, Pallas kernels, on_device(): pl.pallas_call(finish_kernel, out_shape=[jax.ShapeDtypeStruct((3, atoms),...  0.93 us

profile of v6, /device:TPU:0, one launch (start us, length us, event | category | flops | bytes accessed | tf_op | source)
XLA Modules:
  0.0 34.3 jit_solution(4358759461785863383)
XLA Ops:
  1.3 32.1 %shard_map.176 = (f32[3,384]{1,0:T(4,128)S(1)}, bf16[8,32,768]{2,1,0:T(8,128)(2,1)S(1)}) custom-call(f32[384,128]{1,0:T(8,128)} %atom_hbm.1, f32[3,384]{1,0:T(4,128)} %noisy_hbm.1, f32[1]{0:T(128)S(6)} %copy.19.noise_ref, s32[384]{0:T(512)} %ids_hbm.1, f32[256,768]{1,0:T(8,128)} %tok_hbm.1, bf16[256,128,128]{2,1,0:T(8,128)(2,1)} %pair_hbm.1, ...), custom_call_target="tpu_custom_call" | custom-call | tf_op jit(solution)/shard_map/pallas_call | solution.py:698
  33.4 0.9 %shard_map.177 = (f32[3,384]{1,0:T(4,128)}, f32[256,768]{1,0:T(8,128)}) custom-call(bf16[256,768]{1,0:T(8,128)(2,1)S(1)} %bitcast.1, f32[3,384]{1,0:T(4,128)S(1)} %get-tuple-element.5.den_ref), custom_call_target="tpu_custom_call" | custom-call | tf_op jit(solution)/shard_map/pallas_call | solution.py:768
